TPU v7x, 1024 devices: a whole 4x8x16 slice. The times are simulated.
1024 devices in a mesh: dp: 32 (over z_lo, y), tensor: 32 (over z_hi, x, core).
Axes of the slice: x: 4, y: 8, z: 16 (z_hi: 4, z_lo: 4; z = z_hi * 4 + z_lo), core: 2. Of those that a mesh axis runs over, the one named last changes fastest.
Arguments:
- local_gate: bfloat16 [14336, 16384], P('tensor', 'dp'), may hold values from -6 to 6
- local_up: bfloat16 [14336, 16384], P('tensor', 'dp'), may hold values from -6 to 6
- local_grad: bfloat16 [16384, 4096], P('dp'), may hold values from -48 to 48
- orphan_gate: bfloat16 [14336, 1024], P('tensor', 'dp'), may hold values from -6 to 6
- orphan_up: bfloat16 [14336, 1024], P('tensor', 'dp'), may hold values from -6 to 6
- orphan_grad: bfloat16 [1024, 4096], P('dp'), may hold values from -48 to 48
- orphan_len: int32 [32], P('dp'), may hold values from 1 to 32, 896 in all
- orphan_dest: int32 [1024, 1], P('dp'), may hold values from 0 to 31; in each aligned block of 32 rows (0 to 31, 32 to 63, ...) at most 2 rows name the same one
- loop_order: int32 [32], replicated, may hold values from 0 to 31, each once
Outputs:
- down_grad: float32 [14336, 4096], P('tensor', 'dp')
- orphan_load: float32 [32], P('dp')
Inputs may be any that keep to these rules, and one draw needn't show every extreme that they name: `orphan_dest`: among the 32 rows of one holder, at most 2 name the same replica, live or not, and some holder's rows reach 2 for some replica. `loop_order`: A permutation of the replicas.
All inputs are finite; a program needn't handle non-finite values. No bound on the sum of `orphan_len` on one device may be relied on, other than what follows from the above.
Results may differ from a plain program's by a relative error of at most 0.0041.
Values may be sent and summed in bfloat16 or wider, within the bound.
No kernel may reach another device: no remote copies, remote signals or barrier semaphores. Data moves between devices by JAX's collectives and lax.ppermute only.
A program may use at most 32 MiB of HBM per device.

v0:
```python
import jax
import jax.numpy as jnp
from jax import lax
from jax.experimental import pallas as pl
from jax.experimental.pallas import tpu as pltpu
from jax.sharding import Mesh
from jax.sharding import PartitionSpec as P


DP = ("dp_0", "dp_1")
UP_ROWS = 256
SMEM = pl.BlockSpec(memory_space=pltpu.SMEM)
VMEM = pl.BlockSpec(memory_space=pltpu.VMEM)


def room(mib):
    return pltpu.CompilerParams(vmem_limit_bytes=mib * 2**20)


def hidden_of(gate, upper):
    gate = gate.astype(jnp.float32)
    return gate / (1.0 + jnp.exp(-gate)) * upper.astype(jnp.float32)


def first_message(order, place, gate, up, o_gate, o_up, grad, o_grad):
    rows, depth = gate.shape
    outer, inner = lax.axis_size("dp_0"), lax.axis_size("dp_1")
    cols = grad.shape[1] // (outer * inner)
    orphans = o_gate.shape[0]
    half, far = UP_ROWS, inner // 2

    def kernel(order_ref, place_ref, gate_ref, up_ref, o_gate_ref, o_up_ref, *refs):
        grad_refs, o_grad_refs = refs[:outer], refs[outer : 2 * outer]
        hidden_ref, *messages = refs[2 * outer :]
        hidden_ref[:, :depth] = hidden_of(gate_ref[...], up_ref[...]).astype(jnp.bfloat16)
        extra = hidden_of(o_gate_ref[...], o_up_ref[...])
        hidden_ref[:, depth:] = extra.T.astype(jnp.bfloat16)
        for first in range(0, outer, 2):
            both = jnp.concatenate([grad_refs[first][...], grad_refs[first + 1][...]], axis=1)
            term = jnp.dot(hidden_ref[:, :depth], both, preferred_element_type=jnp.float32)
            for k in range(2):
                part = term[:, k * cols : (k + 1) * cols].astype(jnp.bfloat16)
                messages[0][first + k, :half] = part[:half]
                messages[1][first + k, : rows - half] = part[half:]
        for message, start, stop in ((messages[0], 0, half), (messages[1], half, rows)):
            at = stop - start
            for z in range(outer):
                message[z, at : at + orphans] = o_grad_refs[z][...]
                piece = extra[:, min(start + z * cols, stop) : min(start + (z + 1) * cols, stop)]
                piece = piece.astype(jnp.bfloat16)
                if piece.shape[1] < cols:
                    gap = jnp.zeros((orphans, cols - piece.shape[1]), jnp.bfloat16)
                    piece = jnp.concatenate([piece, gap], axis=1) if piece.shape[1] else gap
                message[z, at + orphans :] = piece

    def column_block(height, z):
        def at(turn, order_ref, place_ref):
            return 0, order_ref[z * inner + lax.rem(place_ref[0] + far, inner)]

        return pl.BlockSpec((height, cols), at)

    def whole(*shape):
        return pl.BlockSpec(shape, lambda turn, *_: (0,) * len(shape))

    shapes = [
        (rows, depth + orphans),
        (outer, half + 2 * orphans, cols),
        (outer, rows - half + 2 * orphans, cols),
    ]
    return pl.pallas_call(
        kernel,
        name="first_message",
        out_shape=[jax.ShapeDtypeStruct(shape, jnp.bfloat16) for shape in shapes],
        grid_spec=pltpu.PrefetchScalarGridSpec(
            num_scalar_prefetch=2,
            grid=(1,),
            in_specs=[whole(*gate.shape)] * 2
            + [whole(*o_gate.shape)] * 2
            + [column_block(depth, z) for z in range(outer)]
            + [column_block(orphans, z) for z in range(outer)],
            out_specs=[whole(*shape) for shape in shapes],
        ),
        cost_estimate=pl.CostEstimate(
            flops=2 * rows * depth * outer * cols,
            bytes_accessed=8 * rows * depth,
            transcendentals=rows * depth,
        ),
    )(order, place, gate, up, o_gate, o_up, *[grad] * outer, *[o_grad] * outer)


def other_terms(order, place, names, hidden, grad, o_grad):
    rows, _ = hidden.shape
    own_rows, _ = grad.shape
    outer, inner = lax.axis_size("dp_0"), lax.axis_size("dp_1")
    replicas = outer * inner
    orphans = o_grad.shape[0]
    cols = grad.shape[1] // replicas

    def kernel(
        order_ref, place_ref, names_ref, hidden_ref, grad_ref, o_grad_ref,
        ring_ref, weight_ref, load_ref, up_ref, down_ref,
    ):
        names = names_ref[...].T
        lanes = lax.broadcasted_iota(jnp.int32, (orphans, replicas), 1)
        marks = lanes.astype(jnp.float32)
        taken = jnp.zeros((orphans, replicas), jnp.float32)
        for holder in range(replicas):
            taken = taken + (names[:, holder : holder + 1] == marks).astype(jnp.float32)
        taken = jnp.sum(taken, axis=0, keepdims=True)
        weights = 1.0 / (own_rows + taken)
        line = place_ref[1] - place_ref[0]
        holders = [
            place_ref[1],
            line + lax.rem(place_ref[0] + inner - 1, inner),
            line + lax.rem(place_ref[0] + 1, inner),
        ]

        def entry(row, holder):
            return jnp.sum(jnp.where(lanes[:1] == holder, row, 0.0), axis=1, keepdims=True)

        load_ref[...] = entry(taken, holders[0]) / orphans
        factors = []
        for k, holder in enumerate(holders):
            weight_ref[k : k + 1] = jnp.broadcast_to(entry(weights, holder), (1, cols))
            column = jnp.sum(jnp.where(lanes == holder, names, 0.0), axis=1, keepdims=True)
            factors.append(
                jnp.sum(jnp.where(column == marks, weights, 0.0), axis=1, keepdims=True)
            )
        up_ref[...] = jnp.broadcast_to(factors[1], up_ref.shape)
        down_ref[...] = jnp.broadcast_to(factors[2], down_ref.shape)
        own_weight = weight_ref[:1]

        for turn in range(inner - 1):
            away = turn + 1 + (turn + 1) // (inner // 2)
            to = lax.rem(place_ref[0] + away, inner)

            def block(z):
                at = pl.ds(pl.multiple_of(order_ref[z * inner + to] * cols, cols), cols)
                own = grad_ref[:, at].astype(jnp.float32) * own_weight
                extra = o_grad_ref[:, at].astype(jnp.float32) * factors[0]
                return jnp.concatenate([own.astype(jnp.bfloat16), extra.astype(jnp.bfloat16)], axis=0)

            for first in range(0, outer, 2):
                both = jnp.concatenate([block(first), block(first + 1)], axis=1)
                term = jnp.dot(hidden_ref[...], both, preferred_element_type=jnp.float32)
                for k in range(2):
                    ring_ref[turn, first + k] = term[:, k * cols : (k + 1) * cols]

    return pl.pallas_call(
        kernel,
        name="other_terms",
        out_shape=(
            jax.ShapeDtypeStruct((inner - 1, outer, rows, cols), jnp.float32),
            jax.ShapeDtypeStruct((3, cols), jnp.float32),
            jax.ShapeDtypeStruct((1, 1), jnp.float32),
            jax.ShapeDtypeStruct((orphans, cols), jnp.float32),
            jax.ShapeDtypeStruct((orphans, cols), jnp.float32),
        ),
        in_specs=[SMEM] * 2 + [VMEM] * 4,
        out_specs=(VMEM,) * 5,
        compiler_params=room(20),
        cost_estimate=pl.CostEstimate(
            flops=2 * rows * hidden.shape[1] * grad.shape[1],
            bytes_accessed=2 * hidden.shape[1] * grad.shape[1] + 4 * rows * grad.shape[1],
            transcendentals=0,
        ),
    )(order, place, names, hidden, grad, o_grad)


def ring_sum(away, ring, received, first=None):
    inner, outer, rows, cols = ring.shape[0] + 1, *ring.shape[1:]
    at = (away - 1 - away // (inner // 2)) % inner if away else inner - 2
    operands = [*received, *([] if first is None else [first[0], first[2]])]

    def kernel(ring_ref, *refs):
        came, (out_ref, own_ref, sem) = refs[: len(operands)], refs[len(operands) :]
        copy = pltpu.make_async_copy(ring_ref.at[at], own_ref, sem)
        copy.start()
        if first is not None:
            message, weight_ref, factor_ref = came
            orphans = factor_ref.shape[0]
            count = message.shape[1] - 2 * orphans
            pieces = [message[z, count + orphans :] for z in range(-(-count // cols))]
            theirs = jnp.concatenate(pieces, axis=1).astype(jnp.float32).T
            theirs = theirs[:count].astype(jnp.bfloat16)
        copy.wait()
        for z in range(outer):
            if first is None:
                total = own_ref[z]
                for c in came:
                    total = total + c[z].astype(jnp.float32)
                out_ref[z] = total.astype(jnp.bfloat16)
                continue
            _, row, _, start = first
            scaled = message[z, count : count + orphans].astype(jnp.float32) * factor_ref[...]
            part = message[z, :count].astype(jnp.float32) * weight_ref[row : row + 1]
            part = part + jnp.dot(
                theirs, scaled.astype(jnp.bfloat16), preferred_element_type=jnp.float32
            )
            out_ref[z] = own_ref[z].astype(jnp.bfloat16)
            part = own_ref[z, start : start + count] + part
            out_ref[z, start : start + count] = part.astype(jnp.bfloat16)

    return pl.pallas_call(
        kernel,
        out_shape=jax.ShapeDtypeStruct((outer, rows, cols), jnp.bfloat16),
        in_specs=[pl.BlockSpec(memory_space=pl.ANY)] + [VMEM] * len(operands),
        out_specs=VMEM,
        scratch_shapes=[pltpu.VMEM((outer, rows, cols), jnp.float32), pltpu.SemaphoreType.DMA],
        compiler_params=room(6),
        cost_estimate=pl.CostEstimate(
            flops=2 * outer * rows * cols,
            bytes_accessed=8 * outer * rows * cols,
            transcendentals=0,
        ),
    )(ring, *operands)


def total_of(near):
    outer, rows, cols = near.shape

    def kernel(near_ref, out_ref):
        whole = near_ref[0].astype(jnp.float32)
        for k in range(1, outer):
            whole = whole + near_ref[k].astype(jnp.float32)
        out_ref[...] = whole

    return pl.pallas_call(
        kernel,
        name="total_of",
        out_shape=jax.ShapeDtypeStruct((rows, cols), jnp.float32),
        in_specs=[VMEM],
        out_specs=VMEM,
        compiler_params=room(4),
    )(near)


def shifted(array, by):
    size = lax.axis_size("dp_1")
    return lax.ppermute(array, "dp_1", [(i, (i + by) % size) for i in range(size)])


def exchanged(array, axis):
    return lax.all_to_all(array, axis, split_axis=0, concat_axis=0, tiled=True)


def per_device(
    local_gate,
    local_up,
    local_grad,
    orphan_gate,
    orphan_up,
    orphan_grad,
    orphan_len,
    orphan_dest,
    loop_order,
):
    replicas = lax.axis_size(DP)
    inner = lax.axis_size("dp_1")
    me = lax.axis_index(DP).astype(jnp.int32)
    place = jnp.stack([lax.axis_index("dp_1").astype(jnp.int32), me])
    orphans = orphan_grad.shape[0]
    live = jnp.arange(orphans, dtype=jnp.int32) < orphan_len[0]
    names = jnp.where(live, orphan_dest[:, 0], -1).astype(jnp.float32)
    names = jnp.broadcast_to(names[None, None], (replicas, 1, orphans))
    names = exchanged(names, DP)
    hidden, up, down = first_message(
        loop_order,
        place,
        local_gate,
        local_up,
        orphan_gate.T,
        orphan_up.T,
        local_grad,
        orphan_grad,
    )
    up, down = shifted(up, 1), shifted(down, -1)
    ring, weight, load, up_factor, down_factor = other_terms(
        loop_order, place, names.reshape(replicas, orphans), hidden, local_grad, orphan_grad
    )
    ups, downs = (weight, 1, up_factor, 0), (weight, 2, down_factor, UP_ROWS)
    for away in range(inner // 2 - 1, 0, -1):
        up = shifted(ring_sum(away, ring, [up], ups), 1)
        down = shifted(ring_sum(inner - away, ring, [down], downs), -1)
        ups = downs = None
    near = ring_sum(0, ring, [up, down])
    return total_of(exchanged(near, "dp_0")), load.reshape(1)


def solution(mesh):
    torus = Mesh(mesh.devices.reshape(4, 8, mesh.shape["tensor"]), ("dp_0", "dp_1", "tensor"))

    return jax.shard_map(
        per_device,
        mesh=torus,
        in_specs=(
            P("tensor", DP),
            P("tensor", DP),
            P(DP, None),
            P("tensor", DP),
            P("tensor", DP),
            P(DP, None),
            P(DP),
            P(DP, None),
            P(),
        ),
        out_specs=(P("tensor", DP), P(DP)),
        check_vma=False,
    )
```

profile of v0, /device:TPU:64, one launch (start us, length us, event | category | flops | bytes accessed | tf_op | source)
XLA Modules:
  0.0 96.4 jit_solution(13610090595502178044)
XLA Ops:
  0.6 0.6 pad_add_fusion.place_ref
  1.3 0.0 copy-start.5
  1.3 0.0 copy-start.1
  1.3 0.0 copy-start.2
  1.3 0.0 copy-start.3
  1.3 3.6 %first_message.1 = (bf16[448,544]{1,0:T(8,128)(2,1)}, bf16[4,320,128]{2,1,0:T(8,128)(2,1)}, bf16[4,256,128]{2,1,0:T(8,128)(2,1)}) custom-call(s32[32]{0:T(128)} %order_ref.3, s32[2]{0:T(128)} %pad_add_fusion.place_ref, bf16[448,512]{1,0:T(8,128)(2,1)} %gate_ref.1, bf16[448,512]{1,0:T(8,128)(2,1)} %up_ref.1, bf16[32,448]{1,0:T(8,128)(2,1)} %bitcast.11, ...), custom_call_target="tpu_custom_call" | custom-call | flops 234881024 | bytes 1835008 | tf_op jit(solution)/shard_map/first_message/pallas_call | solution.py:70
  4.9 5.4 %collective-permute-start.4 = (bf16[4,256,128]{2,1,0:T(8,128)(2,1)}, bf16[4,256,128]{2,1,0:T(8,128)(2,1)S(1)}, u32[]{:S(2)}, u32[]{:S(2)}) collective-permute-start(bf16[4,256,128]{2,1,0:T(8,128)(2,1)} %get-tuple-element.15), channel_id=1, source_target_pairs={{0,224},{32,0},{64,32},{96,64},{128,96},{160,128},{192,160},{224,1... | collective-permute-start | bytes 786440 | tf_op jit(solution)/shard_map/ppermute | solution.py:240
  10.3 1.9 %collective-permute-start = (bf16[4,320,128]{2,1,0:T(8,128)(2,1)}, bf16[4,320,128]{2,1,0:T(8,128)(2,1)S(1)}, u32[]{:S(2)}, u32[]{:S(2)}) collective-permute-start(bf16[4,320,128]{2,1,0:T(8,128)(2,1)} %get-tuple-element.12), channel_id=1, source_target_pairs={{0,32},{32,64},{64,96},{96,128},{128,160},{160,192},{192,224},{224... | collective-permute-start | bytes 983048 | tf_op jit(solution)/shard_map/ppermute | solution.py:240
  12.9 0.0 copy-done.5
  12.9 22.5 %all_to_all.10 = f32[32,1,32]{2,1,0:T(1,128)S(1)} all-to-all(f32[32,1,32]{2,1,0:T(1,128)S(1)} %broadcast_in_dim.11), channel_id=1, replica_groups=mesh['dp_0'=4,'dp_1'=8,'tensor'=32] {'dp_0','dp_1'}, dimensions={0} | all-to-all | bytes 8192 | tf_op jit(solution)/shard_map/all_to_all | solution.py:244
  35.4 0.0 copy-done.1
  35.4 0.0 copy-done.2
  35.4 0.0 copy-done.3
  35.4 0.0 copy-start
  35.4 2.2 %copy-done = bf16[512,4096]{1,0:T(8,128)(2,1)S(1)} copy-done((bf16[512,4096]{1,0:T(8,128)(2,1)S(1)}, bf16[512,4096]{1,0:T(8,128)(2,1)}, u32[]{:S(2)}) %copy-start) | copy-done | bytes 4194328
  37.6 0.0 copy-start.4
  37.6 1.1 %copy-done.4 = bf16[448,544]{1,0:T(8,128)(2,1)S(1)} copy-done((bf16[448,544]{1,0:T(8,128)(2,1)S(1)}, bf16[448,544]{1,0:T(8,128)(2,1)}, u32[]{:S(2)}) %copy-start.4) | copy-done | bytes 487448
  38.7 3.9 %other_terms.1 = (f32[7,4,448,128]{3,2,1,0:T(8,128)S(1)}, f32[3,128]{1,0:T(4,128)S(1)}, f32[1,1]{1,0:T(1,128)}, f32[32,128]{1,0:T(8,128)S(1)}, f32[32,128]{1,0:T(8,128)S(1)}) custom-call(s32[32]{0:T(128)S(1)} %copy-done.2, s32[2]{0:T(128)S(1)} %copy-done.3, f32[32,32]{1,0:T(8,128)S(1)} %bitcast.10, bf16[448,544]{1,0:T(8,128)(2,1)S(1)} %copy-done.4, ...), custom_call_target="tpu_custom_call" | custom-call | flops 1996488704 | bytes 11796480 | tf_op jit(solution)/shard_map/other_terms/pallas_call | solution.py:149
  42.5 0.0 collective-permute-done.4.refs_0_
  42.5 0.5 shard_map.107
  43.1 2.5 %collective-permute-start.5 = (bf16[4,448,128]{2,1,0:T(8,128)(2,1)S(1)}, bf16[4,448,128]{2,1,0:T(8,128)(2,1)S(1)}, u32[]{:S(2)}, u32[]{:S(2)}) collective-permute-start(bf16[4,448,128]{2,1,0:T(8,128)(2,1)S(1)} %shard_map.107), channel_id=1, source_target_pairs={{0,224},{32,0},{64,32},{96,64},{128,96},{160,128},{192,160},{224,1... | collective-permute-start | bytes 1376264 | tf_op jit(solution)/shard_map/ppermute | solution.py:240
  45.6 0.0 collective-permute-done.refs_0_
  45.6 0.6 shard_map.104
  46.2 3.4 %collective-permute-start.1 = (bf16[4,448,128]{2,1,0:T(8,128)(2,1)S(1)}, bf16[4,448,128]{2,1,0:T(8,128)(2,1)S(1)}, u32[]{:S(2)}, u32[]{:S(2)}) collective-permute-start(bf16[4,448,128]{2,1,0:T(8,128)(2,1)S(1)} %shard_map.104), channel_id=1, source_target_pairs={{0,32},{32,64},{64,96},{96,128},{128,160},{160,192},{192,224},{224... | collective-permute-start | bytes 1376264 | tf_op jit(solution)/shard_map/ppermute | solution.py:240
  49.5 5.3 %collective-permute-done.5.refs_0_ = bf16[4,448,128]{2,1,0:T(8,128)(2,1)S(1)} collective-permute-done((bf16[4,448,128]{2,1,0:T(8,128)(2,1)S(1)}, bf16[4,448,128]{2,1,0:T(8,128)(2,1)S(1)}, u32[]{:S(2)}, u32[]{:S(2)}) %collective-permute-start.5) | collective-permute-done | bytes 458784 | tf_op jit(solution)/shard_map/ppermute | solution.py:240
  54.8 0.3 shard_map.108
  55.1 2.5 %collective-permute-start.6 = (bf16[4,448,128]{2,1,0:T(8,128)(2,1)S(1)}, bf16[4,448,128]{2,1,0:T(8,128)(2,1)S(1)}, u32[]{:S(2)}, u32[]{:S(2)}) collective-permute-start(bf16[4,448,128]{2,1,0:T(8,128)(2,1)S(1)} %shard_map.108), channel_id=1, source_target_pairs={{0,224},{32,0},{64,32},{96,64},{128,96},{160,128},{192,160},{224,1... | collective-permute-start | bytes 1376264 | tf_op jit(solution)/shard_map/ppermute | solution.py:240
  57.6 0.5 collective-permute-done.1.refs_0_
  58.2 0.3 shard_map.105
  58.5 3.1 %collective-permute-start.2 = (bf16[4,448,128]{2,1,0:T(8,128)(2,1)S(1)}, bf16[4,448,128]{2,1,0:T(8,128)(2,1)S(1)}, u32[]{:S(2)}, u32[]{:S(2)}) collective-permute-start(bf16[4,448,128]{2,1,0:T(8,128)(2,1)S(1)} %shard_map.105), channel_id=1, source_target_pairs={{0,32},{32,64},{64,96},{96,128},{128,160},{160,192},{192,224},{224... | collective-permute-start | bytes 1376264 | tf_op jit(solution)/shard_map/ppermute | solution.py:240
  61.6 6.4 %collective-permute-done.6.refs_0_ = bf16[4,448,128]{2,1,0:T(8,128)(2,1)S(1)} collective-permute-done((bf16[4,448,128]{2,1,0:T(8,128)(2,1)S(1)}, bf16[4,448,128]{2,1,0:T(8,128)(2,1)S(1)}, u32[]{:S(2)}, u32[]{:S(2)}) %collective-permute-start.6) | collective-permute-done | bytes 458784 | tf_op jit(solution)/shard_map/ppermute | solution.py:240
  67.9 0.3 shard_map.109
  68.2 2.6 %collective-permute-start.7 = (bf16[4,448,128]{2,1,0:T(8,128)(2,1)S(1)}, bf16[4,448,128]{2,1,0:T(8,128)(2,1)S(1)}, u32[]{:S(2)}, u32[]{:S(2)}) collective-permute-start(bf16[4,448,128]{2,1,0:T(8,128)(2,1)S(1)} %shard_map.109), channel_id=1, source_target_pairs={{0,224},{32,0},{64,32},{96,64},{128,96},{160,128},{192,160},{224,1... | collective-permute-start | bytes 1376264 | tf_op jit(solution)/shard_map/ppermute | solution.py:240
  70.8 0.8 collective-permute-done.2.refs_0_
  71.7 0.3 shard_map.106
  72.0 2.5 %collective-permute-start.3 = (bf16[4,448,128]{2,1,0:T(8,128)(2,1)S(1)}, bf16[4,448,128]{2,1,0:T(8,128)(2,1)S(1)}, u32[]{:S(2)}, u32[]{:S(2)}) collective-permute-start(bf16[4,448,128]{2,1,0:T(8,128)(2,1)S(1)} %shard_map.106), channel_id=1, source_target_pairs={{0,32},{32,64},{64,96},{96,128},{128,160},{160,192},{192,224},{224... | collective-permute-start | bytes 1376264 | tf_op jit(solution)/shard_map/ppermute | solution.py:240
  74.5 4.1 %collective-permute-done.7.refs_1_ = bf16[4,448,128]{2,1,0:T(8,128)(2,1)S(1)} collective-permute-done((bf16[4,448,128]{2,1,0:T(8,128)(2,1)S(1)}, bf16[4,448,128]{2,1,0:T(8,128)(2,1)S(1)}, u32[]{:S(2)}, u32[]{:S(2)}) %collective-permute-start.7) | collective-permute-done | bytes 458784 | tf_op jit(solution)/shard_map/ppermute | solution.py:240
  78.6 5.0 %collective-permute-done.3.refs_0_ = bf16[4,448,128]{2,1,0:T(8,128)(2,1)S(1)} collective-permute-done((bf16[4,448,128]{2,1,0:T(8,128)(2,1)S(1)}, bf16[4,448,128]{2,1,0:T(8,128)(2,1)S(1)}, u32[]{:S(2)}, u32[]{:S(2)}) %collective-permute-start.3) | collective-permute-done | bytes 458784 | tf_op jit(solution)/shard_map/ppermute | solution.py:240
  83.6 0.4 shard_map.110
  83.9 11.8 %all_to_all.11.near_ref = bf16[4,448,128]{2,1,0:T(8,128)(2,1)S(1)} all-to-all(bf16[4,448,128]{2,1,0:T(8,128)(2,1)S(1)} %shard_map.110), channel_id=1, replica_groups=mesh['dp_0'=4,'dp_1'=8,'tensor'=32] {'dp_0'}, dimensions={0} | all-to-all | bytes 917504 | tf_op jit(solution)/shard_map/all_to_all | solution.py:244
  95.7 0.7 total_of.1
  (2 shorter events, 0.0 us)
Async XLA Ops:
  1.3 11.6 %copy-start.5 = (s32[32,1]{0,1:T(1,128)S(1)}, s32[32,1]{0,1:T(1,128)}, u32[]{:S(2)}) copy-start(s32[32,1]{0,1:T(1,128)} %param.16) | copy-start | bytes 388
  1.3 34.1 %copy-start.1 = (bf16[32,4096]{1,0:T(8,128)(2,1)S(1)}, bf16[32,4096]{1,0:T(8,128)(2,1)}, u32[]{:S(2)}) copy-start(bf16[32,4096]{1,0:T(8,128)(2,1)} %o_grad_ref.1) | copy-start | bytes 786436
  1.3 34.1 %copy-start.2 = (s32[32]{0:T(128)S(1)}, s32[32]{0:T(128)}, u32[]{:S(2)}) copy-start(s32[32]{0:T(128)} %order_ref.3) | copy-start | bytes 388
  1.3 34.1 %copy-start.3 = (s32[2]{0:T(128)S(1)}, s32[2]{0:T(128)}, u32[]{:S(2)}) copy-start(s32[2]{0:T(128)} %pad_add_fusion.place_ref) | copy-start | bytes 28
  4.9 37.6 %collective-permute-start.4 = (bf16[4,256,128]{2,1,0:T(8,128)(2,1)}, bf16[4,256,128]{2,1,0:T(8,128)(2,1)S(1)}, u32[]{:S(2)}, u32[]{:S(2)}) collective-permute-start(bf16[4,256,128]{2,1,0:T(8,128)(2,1)} %get-tuple-element.15), channel_id=1, source_target_pairs={{0,224},{32,0},{64,32},{96,64},{128,96},{160,128},{192,160},{224,1... | collective-permute-start | bytes 786440 | tf_op jit(solution)/shard_map/ppermute | solution.py:240
  10.3 35.3 %collective-permute-start = (bf16[4,320,128]{2,1,0:T(8,128)(2,1)}, bf16[4,320,128]{2,1,0:T(8,128)(2,1)S(1)}, u32[]{:S(2)}, u32[]{:S(2)}) collective-permute-start(bf16[4,320,128]{2,1,0:T(8,128)(2,1)} %get-tuple-element.12), channel_id=1, source_target_pairs={{0,32},{32,64},{64,96},{96,128},{128,160},{160,192},{192,224},{224... | collective-permute-start | bytes 983048 | tf_op jit(solution)/shard_map/ppermute | solution.py:240
  35.4 2.2 %copy-start = (bf16[512,4096]{1,0:T(8,128)(2,1)S(1)}, bf16[512,4096]{1,0:T(8,128)(2,1)}, u32[]{:S(2)}) copy-start(bf16[512,4096]{1,0:T(8,128)(2,1)} %grad_ref.1) | copy-start | bytes 12582916
  37.6 1.1 %copy-start.4 = (bf16[448,544]{1,0:T(8,128)(2,1)S(1)}, bf16[448,544]{1,0:T(8,128)(2,1)}, u32[]{:S(2)}) copy-start(bf16[448,544]{1,0:T(8,128)(2,1)} %get-tuple-element.10.hidden_ref) | copy-start | bytes 1462276
  43.1 11.7 %collective-permute-start.5 = (bf16[4,448,128]{2,1,0:T(8,128)(2,1)S(1)}, bf16[4,448,128]{2,1,0:T(8,128)(2,1)S(1)}, u32[]{:S(2)}, u32[]{:S(2)}) collective-permute-start(bf16[4,448,128]{2,1,0:T(8,128)(2,1)S(1)} %shard_map.107), channel_id=1, source_target_pairs={{0,224},{32,0},{64,32},{96,64},{128,96},{160,128},{192,160},{224,1... | collective-permute-start | bytes 1376264 | tf_op jit(solution)/shard_map/ppermute | solution.py:240
  46.2 12.0 %collective-permute-start.1 = (bf16[4,448,128]{2,1,0:T(8,128)(2,1)S(1)}, bf16[4,448,128]{2,1,0:T(8,128)(2,1)S(1)}, u32[]{:S(2)}, u32[]{:S(2)}) collective-permute-start(bf16[4,448,128]{2,1,0:T(8,128)(2,1)S(1)} %shard_map.104), channel_id=1, source_target_pairs={{0,32},{32,64},{64,96},{96,128},{128,160},{160,192},{192,224},{224... | collective-permute-start | bytes 1376264 | tf_op jit(solution)/shard_map/ppermute | solution.py:240
  55.1 12.8 %collective-permute-start.6 = (bf16[4,448,128]{2,1,0:T(8,128)(2,1)S(1)}, bf16[4,448,128]{2,1,0:T(8,128)(2,1)S(1)}, u32[]{:S(2)}, u32[]{:S(2)}) collective-permute-start(bf16[4,448,128]{2,1,0:T(8,128)(2,1)S(1)} %shard_map.108), channel_id=1, source_target_pairs={{0,224},{32,0},{64,32},{96,64},{128,96},{160,128},{192,160},{224,1... | collective-permute-start | bytes 1376264 | tf_op jit(solution)/shard_map/ppermute | solution.py:240
  58.5 13.2 %collective-permute-start.2 = (bf16[4,448,128]{2,1,0:T(8,128)(2,1)S(1)}, bf16[4,448,128]{2,1,0:T(8,128)(2,1)S(1)}, u32[]{:S(2)}, u32[]{:S(2)}) collective-permute-start(bf16[4,448,128]{2,1,0:T(8,128)(2,1)S(1)} %shard_map.105), channel_id=1, source_target_pairs={{0,32},{32,64},{64,96},{96,128},{128,160},{160,192},{192,224},{224... | collective-permute-start | bytes 1376264 | tf_op jit(solution)/shard_map/ppermute | solution.py:240
  68.2 10.4 %collective-permute-start.7 = (bf16[4,448,128]{2,1,0:T(8,128)(2,1)S(1)}, bf16[4,448,128]{2,1,0:T(8,128)(2,1)S(1)}, u32[]{:S(2)}, u32[]{:S(2)}) collective-permute-start(bf16[4,448,128]{2,1,0:T(8,128)(2,1)S(1)} %shard_map.109), channel_id=1, source_target_pairs={{0,224},{32,0},{64,32},{96,64},{128,96},{160,128},{192,160},{224,1... | collective-permute-start | bytes 1376264 | tf_op jit(solution)/shard_map/ppermute | solution.py:240
  72.0 11.6 %collective-permute-start.3 = (bf16[4,448,128]{2,1,0:T(8,128)(2,1)S(1)}, bf16[4,448,128]{2,1,0:T(8,128)(2,1)S(1)}, u32[]{:S(2)}, u32[]{:S(2)}) collective-permute-start(bf16[4,448,128]{2,1,0:T(8,128)(2,1)S(1)} %shard_map.106), channel_id=1, source_target_pairs={{0,32},{32,64},{64,96},{96,128},{128,160},{160,192},{192,224},{224... | collective-permute-start | bytes 1376264 | tf_op jit(solution)/shard_map/ppermute | solution.py:240
where the time goes:
time: 97 us; the launch traced here: 96.4 us
  blocking collectives  34.2 us (35%)
  starting transfers between devices  23.8 us (25%)
  waiting for transfers between devices  22.1 us (23%)
  Pallas kernels  10.9 us (11%)
  local copies, waits for them, and re-layouts  3.27 us (3%)
  between operations  1.46 us (2%)
    all_to_all x2, blocking collectives, exchanged(): return lax.all_to_all(array, axis, split_axis=0, concat_axis=0, tiled=True)  34.2 us
    ppermute x8, starting transfers between devices, shifted(): lax.ppermute(array, 'dp_1', [(i, (i + by) % size) for i in range(size)])  23.8 us
    ppermute x8, waiting for transfers between devices, shifted(): lax.ppermute(array, 'dp_1', [(i, (i + by) % size) for i in range(size)])  22.1 us
    pallas_call x1, Pallas kernels, other_terms(): pl.pallas_call(kernel, name='other_terms', out_shape=(jax.ShapeDtypeStruc...  3.86 us
    pallas_call x1, Pallas kernels, first_message(): pl.pallas_call(kernel, name='first_message', out_shape=[jax.ShapeDtypeStr...  3.63 us
    unnamed x12, local copies, waits for them, and re-layouts  3.26 us
    pallas_call x7, Pallas kernels, ring_sum(): pl.pallas_call(kernel, out_shape=jax.ShapeDtypeStruct((outer, rows, cols)...  2.69 us
  transfers between devices with their start and end apart: 8, of which 6 were waited for; matrix products, arithmetic and copies ran while one was open for 0% of the time, Pallas kernels for 6%

commit v1 on v0

--- a/solution.py
+++ b/solution.py
@@ -46,11 +46,12 @@
             at = stop - start
             for z in range(outer):
                 message[z, at : at + orphans] = o_grad_refs[z][...]
-                piece = extra[:, min(start + z * cols, stop) : min(start + (z + 1) * cols, stop)]
+                left = start + z % (outer // 2) * cols
+                piece = extra[:, left : min(left + cols, stop)]
                 piece = piece.astype(jnp.bfloat16)
                 if piece.shape[1] < cols:
                     gap = jnp.zeros((orphans, cols - piece.shape[1]), jnp.bfloat16)
-                    piece = jnp.concatenate([piece, gap], axis=1) if piece.shape[1] else gap
+                    piece = jnp.concatenate([piece, gap], axis=1)
                 message[z, at + orphans :] = piece
 
     def column_block(height, z):
@@ -88,7 +89,7 @@
     )(order, place, gate, up, o_gate, o_up, *[grad] * outer, *[o_grad] * outer)
 
 
-def other_terms(order, place, names, hidden, grad, o_grad):
+def other_terms(order, place, me, names, hidden, grad, o_grad):
     rows, _ = hidden.shape
     own_rows, _ = grad.shape
     outer, inner = lax.axis_size("dp_0"), lax.axis_size("dp_1")
@@ -97,7 +98,7 @@
     cols = grad.shape[1] // replicas
 
     def kernel(
-        order_ref, place_ref, names_ref, hidden_ref, grad_ref, o_grad_ref,
+        order_ref, place_ref, me_ref, names_ref, hidden_ref, grad_ref, o_grad_ref,
         ring_ref, weight_ref, load_ref, up_ref, down_ref,
     ):
         names = names_ref[...].T
@@ -108,9 +109,9 @@
             taken = taken + (names[:, holder : holder + 1] == marks).astype(jnp.float32)
         taken = jnp.sum(taken, axis=0, keepdims=True)
         weights = 1.0 / (own_rows + taken)
-        line = place_ref[1] - place_ref[0]
+        line = me_ref[0] - place_ref[0]
         holders = [
-            place_ref[1],
+            me_ref[0],
             line + lax.rem(place_ref[0] + inner - 1, inner),
             line + lax.rem(place_ref[0] + 1, inner),
         ]
@@ -156,7 +157,7 @@
             jax.ShapeDtypeStruct((orphans, cols), jnp.float32),
             jax.ShapeDtypeStruct((orphans, cols), jnp.float32),
         ),
-        in_specs=[SMEM] * 2 + [VMEM] * 4,
+        in_specs=[SMEM] * 3 + [VMEM] * 4,
         out_specs=(VMEM,) * 5,
         compiler_params=room(20),
         cost_estimate=pl.CostEstimate(
@@ -164,47 +165,84 @@
             bytes_accessed=2 * hidden.shape[1] * grad.shape[1] + 4 * rows * grad.shape[1],
             transcendentals=0,
         ),
-    )(order, place, names, hidden, grad, o_grad)
-
-
-def ring_sum(away, ring, received, first=None):
+    )(order, place, me, names, hidden, grad, o_grad)
+
+
+def ring_sum(away, blocks, ring, received, first=None):
     inner, outer, rows, cols = ring.shape[0] + 1, *ring.shape[1:]
     at = (away - 1 - away // (inner // 2)) % inner if away else inner - 2
-    operands = [*received, *([] if first is None else [first[0], first[2]])]
+    base, count = blocks
+    operands = [a for a, _ in received]
+    operands += [] if first is None else [first[0], first[2]]
 
     def kernel(ring_ref, *refs):
         came, (out_ref, own_ref, sem) = refs[: len(operands)], refs[len(operands) :]
-        copy = pltpu.make_async_copy(ring_ref.at[at], own_ref, sem)
+        copy = pltpu.make_async_copy(ring_ref.at[at, pl.ds(base, count)], own_ref, sem)
         copy.start()
         if first is not None:
             message, weight_ref, factor_ref = came
+            offset = received[0][1]
             orphans = factor_ref.shape[0]
-            count = message.shape[1] - 2 * orphans
-            pieces = [message[z, count + orphans :] for z in range(-(-count // cols))]
+            own = message.shape[1] - 2 * orphans
+            pieces = [message[offset + z, own + orphans :] for z in range(outer // 2)]
             theirs = jnp.concatenate(pieces, axis=1).astype(jnp.float32).T
-            theirs = theirs[:count].astype(jnp.bfloat16)
+            theirs = theirs[:own].astype(jnp.bfloat16)
         copy.wait()
-        for z in range(outer):
+        for z in range(count):
             if first is None:
                 total = own_ref[z]
-                for c in came:
-                    total = total + c[z].astype(jnp.float32)
+                for c, (_, offset) in zip(came, received):
+                    total = total + c[offset + z].astype(jnp.float32)
                 out_ref[z] = total.astype(jnp.bfloat16)
                 continue
             _, row, _, start = first
-            scaled = message[z, count : count + orphans].astype(jnp.float32) * factor_ref[...]
-            part = message[z, :count].astype(jnp.float32) * weight_ref[row : row + 1]
+            block = message.at[offset + z]
+            scaled = block[own : own + orphans].astype(jnp.float32) * factor_ref[...]
+            part = block[:own].astype(jnp.float32) * weight_ref[row : row + 1]
             part = part + jnp.dot(
                 theirs, scaled.astype(jnp.bfloat16), preferred_element_type=jnp.float32
             )
             out_ref[z] = own_ref[z].astype(jnp.bfloat16)
-            part = own_ref[z, start : start + count] + part
-            out_ref[z, start : start + count] = part.astype(jnp.bfloat16)
-
-    return pl.pallas_call(
-        kernel,
+            part = own_ref[z, start : start + own] + part
+            out_ref[z, start : start + own] = part.astype(jnp.bfloat16)
+
+    return pl.pallas_call(
+        kernel,
+        out_shape=jax.ShapeDtypeStruct((count, rows, cols), jnp.bfloat16),
+        in_specs=[pl.BlockSpec(memory_space=pl.ANY)] + [VMEM] * len(operands),
+        out_specs=VMEM,
+        scratch_shapes=[pltpu.VMEM((count, rows, cols), jnp.float32), pltpu.SemaphoreType.DMA],
+        compiler_params=room(6),
+        cost_estimate=pl.CostEstimate(
+            flops=2 * count * rows * cols,
+            bytes_accessed=8 * count * rows * cols,
+            transcendentals=0,
+        ),
+    )(ring, *operands)
+
+
+def near_sum(ring, *received):
+    outer, rows, cols = ring.shape[1:]
+
+    def kernel(ring_ref, *refs):
+        came, (out_ref, own_ref, sem) = refs[: len(received)], refs[len(received) :]
+        copy = pltpu.make_async_copy(ring_ref.at[ring.shape[0] - 1], own_ref, sem)
+        copy.start()
+        copy.wait()
+        for z in range(outer):
+            total, at = own_ref[z], 0
+            for c in came:
+                first = at % outer
+                if first <= z < first + c.shape[0]:
+                    total = total + c[z - first].astype(jnp.float32)
+                at += c.shape[0]
+            out_ref[z] = total.astype(jnp.bfloat16)
+
+    return pl.pallas_call(
+        kernel,
+        name="near",
         out_shape=jax.ShapeDtypeStruct((outer, rows, cols), jnp.bfloat16),
-        in_specs=[pl.BlockSpec(memory_space=pl.ANY)] + [VMEM] * len(operands),
+        in_specs=[pl.BlockSpec(memory_space=pl.ANY)] + [VMEM] * len(received),
         out_specs=VMEM,
         scratch_shapes=[pltpu.VMEM((outer, rows, cols), jnp.float32), pltpu.SemaphoreType.DMA],
         compiler_params=room(6),
@@ -213,7 +251,7 @@
             bytes_accessed=8 * outer * rows * cols,
             transcendentals=0,
         ),
-    )(ring, *operands)
+    )(ring, *received)
 
 
 def total_of(near):
@@ -258,15 +296,16 @@
     replicas = lax.axis_size(DP)
     inner = lax.axis_size("dp_1")
     me = lax.axis_index(DP).astype(jnp.int32)
-    place = jnp.stack([lax.axis_index("dp_1").astype(jnp.int32), me])
+    line = lax.axis_index("dp_1").astype(jnp.int32).reshape(1)
+    me = me.reshape(1)
     orphans = orphan_grad.shape[0]
-    live = jnp.arange(orphans, dtype=jnp.int32) < orphan_len[0]
-    names = jnp.where(live, orphan_dest[:, 0], -1).astype(jnp.float32)
-    names = jnp.broadcast_to(names[None, None], (replicas, 1, orphans))
+    live = lax.broadcasted_iota(jnp.int32, (replicas, 1, orphans), 2) < orphan_len[0]
+    names = jnp.broadcast_to(orphan_dest[:, 0][None, None], live.shape)
+    names = jnp.where(live, names, -1).astype(jnp.float32)
     names = exchanged(names, DP)
     hidden, up, down = first_message(
         loop_order,
-        place,
+        line,
         local_gate,
         local_up,
         orphan_gate.T,
@@ -276,14 +315,22 @@
     )
     up, down = shifted(up, 1), shifted(down, -1)
     ring, weight, load, up_factor, down_factor = other_terms(
-        loop_order, place, names.reshape(replicas, orphans), hidden, local_grad, orphan_grad
+        loop_order, line, me, names.reshape(replicas, orphans), hidden, local_grad, orphan_grad
     )
     ups, downs = (weight, 1, up_factor, 0), (weight, 2, down_factor, UP_ROWS)
+    count = lax.axis_size("dp_0") // 2
+    bases = (0, count)
+    up, down = [(up, base) for base in bases], [(down, base) for base in bases]
     for away in range(inner // 2 - 1, 0, -1):
-        up = shifted(ring_sum(away, ring, [up], ups), 1)
-        down = shifted(ring_sum(inner - away, ring, [down], downs), -1)
+        back = inner - away
+        for k, base in enumerate(bases):
+            blocks = base, count
+            sent = ring_sum(away, blocks, ring, [up[k]], ups)
+            up[k] = shifted(sent, 1), 0
+            sent = ring_sum(back, blocks, ring, [down[k]], downs)
+            down[k] = shifted(sent, -1), 0
         ups = downs = None
-    near = ring_sum(0, ring, [up, down])
+    near = near_sum(ring, *[a for a, _ in up], *[a for a, _ in down])
     return total_of(exchanged(near, "dp_0")), load.reshape(1)
 
 

time: 97 us -> 105 us (1.082)
  starting transfers between devices: 23.8 us -> 57.7 us
  blocking collectives: 34.2 us -> 11.8 us
  waiting for transfers between devices: 22.1 us -> 16.1 us
  Pallas kernels: 10.9 us -> 13.4 us
    all_to_all x2 -> x1, blocking collectives: 34.2 us -> 11.8 us  [exchanged(): return lax.all_to_all(array, axis, split_axis=0, concat_axis=0, tiled=True)]
    ppermute x8 -> x14, starting transfers between devices: 23.8 us -> 43.3 us  [shifted(): lax.ppermute(array, 'dp_1', [(i, (i + by) % size) for i in range(size)])]
    ppermute x8 -> x14, waiting for transfers between devices: 22.1 us -> 7.21 us  [shifted(): lax.ppermute(array, 'dp_1', [(i, (i + by) % size) for i in range(size)])]
    all_to_all x0 -> x1, starting transfers between devices: none -> 14.3 us  [exchanged(): return lax.all_to_all(array, axis, split_axis=0, concat_axis=0, tiled=True)]
    all_to_all x0 -> x1, waiting for transfers between devices: none -> 8.91 us  [exchanged(): return lax.all_to_all(array, axis, split_axis=0, concat_axis=0, tiled=True)]
    pallas_call x7 -> x13, Pallas kernels: 2.69 us -> 5.17 us  [the longest x12 4.8 us: ring_sum(): pl.pallas_call(kernel, out_shape=jax.ShapeDtypeStruct((count, rows, cols)...]
    unnamed x12 -> x10, local copies, waits for them, and re-layouts: 3.26 us -> 3.26 us
  transfers between devices with their start and end apart: 8 -> 15, of which waited for: 6 -> 3; matrix products, arithmetic and copies ran while one was open for 0% -> 1% of each run, Pallas kernels for 6% -> 8%
where the time goes in v1:
time: 105 us
  starting transfers between devices  57.7 us (55%)
  waiting for transfers between devices  16.1 us (15%)
  Pallas kernels  13.4 us (13%)
  blocking collectives  11.8 us (11%)
  local copies, waits for them, and re-layouts  3.26 us (3%)
  between operations  1.65 us (2%)
    ppermute x14, starting transfers between devices, shifted(): lax.ppermute(array, 'dp_1', [(i, (i + by) % size) for i in range(size)])  43.3 us
    all_to_all x1, starting transfers between devices, exchanged(): return lax.all_to_all(array, axis, split_axis=0, concat_axis=0, tiled=True)  14.3 us
    all_to_all x1, blocking collectives, exchanged(): return lax.all_to_all(array, axis, split_axis=0, concat_axis=0, tiled=True)  11.8 us
    all_to_all x1, waiting for transfers between devices, exchanged(): return lax.all_to_all(array, axis, split_axis=0, concat_axis=0, tiled=True)  8.91 us
    ppermute x14, waiting for transfers between devices, shifted(): lax.ppermute(array, 'dp_1', [(i, (i + by) % size) for i in range(size)])  7.21 us
    pallas_call x12, Pallas kernels, ring_sum(): pl.pallas_call(kernel, out_shape=jax.ShapeDtypeStruct((count, rows, cols)...  4.8 us
    pallas_call x1, Pallas kernels, other_terms(): pl.pallas_call(kernel, name='other_terms', out_shape=(jax.ShapeDtypeStruc...  3.85 us
    pallas_call x1, Pallas kernels, first_message(): pl.pallas_call(kernel, name='first_message', out_shape=[jax.ShapeDtypeStr...  3.67 us
  transfers between devices with their start and end apart: 15, of which 3 were waited for; matrix products, arithmetic and copies ran while one was open for 1% of the time, Pallas kernels for 8%

profile of v1, /device:TPU:64, one launch (start us, length us, event | category | flops | bytes accessed | tf_op | source)
XLA Modules:
  0.0 104.5 jit_solution(17381731750827845236)
XLA Ops:
  0.6 0.0 copy-start.4
  0.6 0.0 copy-start.1
  0.7 0.0 copy-start.2
  0.7 3.7 %first_message.1 = (bf16[448,544]{1,0:T(8,128)(2,1)}, bf16[4,320,128]{2,1,0:T(8,128)(2,1)}, bf16[4,256,128]{2,1,0:T(8,128)(2,1)}) custom-call(s32[32]{0:T(128)} %order_ref.3, s32[1]{0:T(128)} %bitcast.place_ref, bf16[448,512]{1,0:T(8,128)(2,1)} %gate_ref.1, bf16[448,512]{1,0:T(8,128)(2,1)} %up_ref.1, bf16[32,448]{1,0:T(8,128)(2,1)} %bitcast.10, ...), custom_call_target="tpu_custom_call" | custom-call | flops 234881024 | bytes 1835008 | tf_op jit(solution)/shard_map/first_message/pallas_call | solution.py:71
  4.3 5.4 %collective-permute-start.7 = (bf16[4,256,128]{2,1,0:T(8,128)(2,1)}, bf16[4,256,128]{2,1,0:T(8,128)(2,1)S(1)}, u32[]{:S(2)}, u32[]{:S(2)}) collective-permute-start(bf16[4,256,128]{2,1,0:T(8,128)(2,1)} %get-tuple-element.15), channel_id=1, source_target_pairs={{0,224},{32,0},{64,32},{96,64},{128,96},{160,128},{192,160},{224,1... | collective-permute-start | bytes 786440 | tf_op jit(solution)/shard_map/ppermute | solution.py:278
  9.7 1.9 %collective-permute-start = (bf16[4,320,128]{2,1,0:T(8,128)(2,1)}, bf16[4,320,128]{2,1,0:T(8,128)(2,1)S(1)}, u32[]{:S(2)}, u32[]{:S(2)}) collective-permute-start(bf16[4,320,128]{2,1,0:T(8,128)(2,1)} %get-tuple-element.12), channel_id=1, source_target_pairs={{0,32},{32,64},{64,96},{96,128},{128,160},{160,192},{192,224},{224... | collective-permute-start | bytes 983048 | tf_op jit(solution)/shard_map/ppermute | solution.py:278
  12.3 0.0 copy-done.4
  12.3 0.6 fusion
  12.9 14.3 %all-to-all-start = ((f32[32,1,32]{2,1,0:T(1,128)}), f32[32,1,32]{2,1,0:T(1,128)S(1)}, u32[]{:S(2)}, u32[]{:S(2)}) async-start(f32[32,1,32]{2,1,0:T(1,128)} %fusion), calls=%async_computation | async-start | bytes 32768 | tf_op jit(solution)/shard_map/all_to_all | solution.py:282
  27.3 8.9 %all-to-all-done = f32[32,1,32]{2,1,0:T(1,128)S(1)} async-done(((f32[32,1,32]{2,1,0:T(1,128)}), f32[32,1,32]{2,1,0:T(1,128)S(1)}, u32[]{:S(2)}, u32[]{:S(2)}) %all-to-all-start) | async-done | bytes 4128 | tf_op jit(solution)/shard_map/all_to_all | solution.py:282
  36.2 0.0 copy-done.1
  36.2 0.0 copy-done.2
  36.2 0.0 copy-start
  36.2 2.2 %copy-done = bf16[512,4096]{1,0:T(8,128)(2,1)S(1)} copy-done((bf16[512,4096]{1,0:T(8,128)(2,1)S(1)}, bf16[512,4096]{1,0:T(8,128)(2,1)}, u32[]{:S(2)}) %copy-start) | copy-done | bytes 4194328
  38.4 0.0 copy-start.3
  38.4 1.1 %copy-done.3 = bf16[448,544]{1,0:T(8,128)(2,1)S(1)} copy-done((bf16[448,544]{1,0:T(8,128)(2,1)S(1)}, bf16[448,544]{1,0:T(8,128)(2,1)}, u32[]{:S(2)}) %copy-start.3) | copy-done | bytes 487448
  39.5 3.9 %other_terms.1 = (f32[7,4,448,128]{3,2,1,0:T(8,128)S(1)}, f32[3,128]{1,0:T(4,128)S(1)}, f32[1,1]{1,0:T(1,128)}, f32[32,128]{1,0:T(8,128)S(1)}, f32[32,128]{1,0:T(8,128)S(1)}) custom-call(s32[32]{0:T(128)S(1)} %copy-done.2, s32[1]{0:T(128)} %bitcast.place_ref, s32[1]{0:T(128)} %bitcast.1.me_ref, f32[32,32]{1,0:T(8,128)S(1)} %bitcast.9, ...), custom_call_target="tpu_custom_call" | custom-call | flops 1996488704 | bytes 11796480 | tf_op jit(solution)/shard_map/other_terms/pallas_call | solution.py:150
  43.3 0.0 collective-permute-done.7.refs_0_
  43.3 0.5 shard_map.110
  43.9 2.5 %collective-permute-start.8 = (bf16[2,448,128]{2,1,0:T(8,128)(2,1)S(1)}, bf16[2,448,128]{2,1,0:T(8,128)(2,1)S(1)}, u32[]{:S(2)}, u32[]{:S(2)}) collective-permute-start(bf16[2,448,128]{2,1,0:T(8,128)(2,1)S(1)} %shard_map.110), channel_id=1, source_target_pairs={{0,224},{32,0},{64,32},{96,64},{128,96},{160,128},{192,160},{224,1... | collective-permute-start | bytes 688136 | tf_op jit(solution)/shard_map/ppermute | solution.py:278
  46.4 0.6 shard_map.113
  46.9 2.5 %collective-permute-start.11 = (bf16[2,448,128]{2,1,0:T(8,128)(2,1)S(1)}, bf16[2,448,128]{2,1,0:T(8,128)(2,1)S(1)}, u32[]{:S(2)}, u32[]{:S(2)}) collective-permute-start(bf16[2,448,128]{2,1,0:T(8,128)(2,1)S(1)} %shard_map.113), channel_id=1, source_target_pairs={{0,224},{32,0},{64,32},{96,64},{128,96},{160,128},{192,160},{224,1... | collective-permute-start | bytes 688136 | tf_op jit(solution)/shard_map/ppermute | solution.py:278
  49.4 0.0 collective-permute-done.refs_0_
  49.4 0.6 shard_map.104
  50.0 3.3 %collective-permute-start.1 = (bf16[2,448,128]{2,1,0:T(8,128)(2,1)S(1)}, bf16[2,448,128]{2,1,0:T(8,128)(2,1)S(1)}, u32[]{:S(2)}, u32[]{:S(2)}) collective-permute-start(bf16[2,448,128]{2,1,0:T(8,128)(2,1)S(1)} %shard_map.104), channel_id=1, source_target_pairs={{0,32},{32,64},{64,96},{96,128},{128,160},{160,192},{192,224},{224... | collective-permute-start | bytes 688136 | tf_op jit(solution)/shard_map/ppermute | solution.py:278
  53.4 0.6 shard_map.107
  53.9 3.3 %collective-permute-start.4 = (bf16[2,448,128]{2,1,0:T(8,128)(2,1)S(1)}, bf16[2,448,128]{2,1,0:T(8,128)(2,1)S(1)}, u32[]{:S(2)}, u32[]{:S(2)}) collective-permute-start(bf16[2,448,128]{2,1,0:T(8,128)(2,1)S(1)} %shard_map.107), channel_id=1, source_target_pairs={{0,32},{32,64},{64,96},{96,128},{128,160},{160,192},{192,224},{224... | collective-permute-start | bytes 688136 | tf_op jit(solution)/shard_map/ppermute | solution.py:278
  57.3 0.0 collective-permute-done.8.refs_0_
  57.3 0.3 shard_map.111
  57.6 3.7 %collective-permute-start.9 = (bf16[2,448,128]{2,1,0:T(8,128)(2,1)S(1)}, bf16[2,448,128]{2,1,0:T(8,128)(2,1)S(1)}, u32[]{:S(2)}, u32[]{:S(2)}) collective-permute-start(bf16[2,448,128]{2,1,0:T(8,128)(2,1)S(1)} %shard_map.111), channel_id=1, source_target_pairs={{0,224},{32,0},{64,32},{96,64},{128,96},{160,128},{192,160},{224,1... | collective-permute-start | bytes 688136 | tf_op jit(solution)/shard_map/ppermute | solution.py:278
  61.3 0.0 collective-permute-done.11.refs_0_
  61.4 0.3 shard_map.114
  61.7 2.5 %collective-permute-start.12 = (bf16[2,448,128]{2,1,0:T(8,128)(2,1)S(1)}, bf16[2,448,128]{2,1,0:T(8,128)(2,1)S(1)}, u32[]{:S(2)}, u32[]{:S(2)}) collective-permute-start(bf16[2,448,128]{2,1,0:T(8,128)(2,1)S(1)} %shard_map.114), channel_id=1, source_target_pairs={{0,224},{32,0},{64,32},{96,64},{128,96},{160,128},{192,160},{224,1... | collective-permute-start | bytes 688136 | tf_op jit(solution)/shard_map/ppermute | solution.py:278
  64.2 0.0 collective-permute-done.1.refs_0_
  64.2 0.3 shard_map.105
  64.5 3.3 %collective-permute-start.2 = (bf16[2,448,128]{2,1,0:T(8,128)(2,1)S(1)}, bf16[2,448,128]{2,1,0:T(8,128)(2,1)S(1)}, u32[]{:S(2)}, u32[]{:S(2)}) collective-permute-start(bf16[2,448,128]{2,1,0:T(8,128)(2,1)S(1)} %shard_map.105), channel_id=1, source_target_pairs={{0,32},{32,64},{64,96},{96,128},{128,160},{160,192},{192,224},{224... | collective-permute-start | bytes 688136 | tf_op jit(solution)/shard_map/ppermute | solution.py:278
  67.9 0.0 collective-permute-done.4.refs_0_
  67.9 0.3 shard_map.108
  68.2 2.1 %collective-permute-start.5 = (bf16[2,448,128]{2,1,0:T(8,128)(2,1)S(1)}, bf16[2,448,128]{2,1,0:T(8,128)(2,1)S(1)}, u32[]{:S(2)}, u32[]{:S(2)}) collective-permute-start(bf16[2,448,128]{2,1,0:T(8,128)(2,1)S(1)} %shard_map.108), channel_id=1, source_target_pairs={{0,32},{32,64},{64,96},{96,128},{128,160},{160,192},{192,224},{224... | collective-permute-start | bytes 688136 | tf_op jit(solution)/shard_map/ppermute | solution.py:278
  70.4 0.0 collective-permute-done.9.refs_0_
  70.4 0.3 shard_map.112
  70.7 4.9 %collective-permute-start.10 = (bf16[2,448,128]{2,1,0:T(8,128)(2,1)S(1)}, bf16[2,448,128]{2,1,0:T(8,128)(2,1)S(1)}, u32[]{:S(2)}, u32[]{:S(2)}) collective-permute-start(bf16[2,448,128]{2,1,0:T(8,128)(2,1)S(1)} %shard_map.112), channel_id=1, source_target_pairs={{0,224},{32,0},{64,32},{96,64},{128,96},{160,128},{192,160},{224,1... | collective-permute-start | bytes 688136 | tf_op jit(solution)/shard_map/ppermute | solution.py:278
  75.6 0.0 collective-permute-done.12.refs_0_
  75.7 0.3 shard_map.115
  76.0 2.5 %collective-permute-start.13 = (bf16[2,448,128]{2,1,0:T(8,128)(2,1)S(1)}, bf16[2,448,128]{2,1,0:T(8,128)(2,1)S(1)}, u32[]{:S(2)}, u32[]{:S(2)}) collective-permute-start(bf16[2,448,128]{2,1,0:T(8,128)(2,1)S(1)} %shard_map.115), channel_id=1, source_target_pairs={{0,224},{32,0},{64,32},{96,64},{128,96},{160,128},{192,160},{224,1... | collective-permute-start | bytes 688136 | tf_op jit(solution)/shard_map/ppermute | solution.py:278
  78.5 0.0 collective-permute-done.2.refs_0_
  78.5 0.3 shard_map.106
  78.8 3.3 %collective-permute-start.3 = (bf16[2,448,128]{2,1,0:T(8,128)(2,1)S(1)}, bf16[2,448,128]{2,1,0:T(8,128)(2,1)S(1)}, u32[]{:S(2)}, u32[]{:S(2)}) collective-permute-start(bf16[2,448,128]{2,1,0:T(8,128)(2,1)S(1)} %shard_map.106), channel_id=1, source_target_pairs={{0,32},{32,64},{64,96},{96,128},{128,160},{160,192},{192,224},{224... | collective-permute-start | bytes 688136 | tf_op jit(solution)/shard_map/ppermute | solution.py:278
  82.2 0.0 collective-permute-done.5.refs_0_
  82.2 0.3 shard_map.109
  82.5 1.9 %collective-permute-start.6 = (bf16[2,448,128]{2,1,0:T(8,128)(2,1)S(1)}, bf16[2,448,128]{2,1,0:T(8,128)(2,1)S(1)}, u32[]{:S(2)}, u32[]{:S(2)}) collective-permute-start(bf16[2,448,128]{2,1,0:T(8,128)(2,1)S(1)} %shard_map.109), channel_id=1, source_target_pairs={{0,32},{32,64},{64,96},{96,128},{128,160},{160,192},{192,224},{224... | collective-permute-start | bytes 688136 | tf_op jit(solution)/shard_map/ppermute | solution.py:278
  84.5 0.0 collective-permute-done.10.refs_2_
  84.5 0.0 collective-permute-done.13.refs_3_
  84.5 3.5 %collective-permute-done.3.refs_0_ = bf16[2,448,128]{2,1,0:T(8,128)(2,1)S(1)} collective-permute-done((bf16[2,448,128]{2,1,0:T(8,128)(2,1)S(1)}, bf16[2,448,128]{2,1,0:T(8,128)(2,1)S(1)}, u32[]{:S(2)}, u32[]{:S(2)}) %collective-permute-start.3) | collective-permute-done | bytes 229408 | tf_op jit(solution)/shard_map/ppermute | solution.py:278
  88.0 3.7 %collective-permute-done.6.refs_1_ = bf16[2,448,128]{2,1,0:T(8,128)(2,1)S(1)} collective-permute-done((bf16[2,448,128]{2,1,0:T(8,128)(2,1)S(1)}, bf16[2,448,128]{2,1,0:T(8,128)(2,1)S(1)}, u32[]{:S(2)}, u32[]{:S(2)}) %collective-permute-start.6) | collective-permute-done | bytes 229408 | tf_op jit(solution)/shard_map/ppermute | solution.py:278
  91.6 0.4 near.1
  92.0 11.8 %all_to_all.10.near_ref = bf16[4,448,128]{2,1,0:T(8,128)(2,1)S(1)} all-to-all(bf16[4,448,128]{2,1,0:T(8,128)(2,1)S(1)} %near.1), channel_id=1, replica_groups=mesh['dp_0'=4,'dp_1'=8,'tensor'=32] {'dp_0'}, dimensions={0} | all-to-all | bytes 917504 | tf_op jit(solution)/shard_map/all_to_all | solution.py:282
  103.8 0.7 total_of.1
  (1 shorter events, 0.0 us)
Async XLA Ops:
  0.6 11.7 %copy-start.4 = (s32[32,1]{0,1:T(1,128)S(1)}, s32[32,1]{0,1:T(1,128)}, u32[]{:S(2)}) copy-start(s32[32,1]{0,1:T(1,128)} %param.16) | copy-start | bytes 388
  0.6 35.6 %copy-start.1 = (bf16[32,4096]{1,0:T(8,128)(2,1)S(1)}, bf16[32,4096]{1,0:T(8,128)(2,1)}, u32[]{:S(2)}) copy-start(bf16[32,4096]{1,0:T(8,128)(2,1)} %o_grad_ref.1) | copy-start | bytes 786436
  0.7 35.5 %copy-start.2 = (s32[32]{0:T(128)S(1)}, s32[32]{0:T(128)}, u32[]{:S(2)}) copy-start(s32[32]{0:T(128)} %order_ref.3) | copy-start | bytes 388
  4.3 39.0 %collective-permute-start.7 = (bf16[4,256,128]{2,1,0:T(8,128)(2,1)}, bf16[4,256,128]{2,1,0:T(8,128)(2,1)S(1)}, u32[]{:S(2)}, u32[]{:S(2)}) collective-permute-start(bf16[4,256,128]{2,1,0:T(8,128)(2,1)} %get-tuple-element.15), channel_id=1, source_target_pairs={{0,224},{32,0},{64,32},{96,64},{128,96},{160,128},{192,160},{224,1... | collective-permute-start | bytes 786440 | tf_op jit(solution)/shard_map/ppermute | solution.py:278
  9.7 39.7 %collective-permute-start = (bf16[4,320,128]{2,1,0:T(8,128)(2,1)}, bf16[4,320,128]{2,1,0:T(8,128)(2,1)S(1)}, u32[]{:S(2)}, u32[]{:S(2)}) collective-permute-start(bf16[4,320,128]{2,1,0:T(8,128)(2,1)} %get-tuple-element.12), channel_id=1, source_target_pairs={{0,32},{32,64},{64,96},{96,128},{128,160},{160,192},{192,224},{224... | collective-permute-start | bytes 983048 | tf_op jit(solution)/shard_map/ppermute | solution.py:278
  12.9 23.3 %all-to-all-start = ((f32[32,1,32]{2,1,0:T(1,128)}), f32[32,1,32]{2,1,0:T(1,128)S(1)}, u32[]{:S(2)}, u32[]{:S(2)}) async-start(f32[32,1,32]{2,1,0:T(1,128)} %fusion), calls=%async_computation | async-start | bytes 32768 | tf_op jit(solution)/shard_map/all_to_all | solution.py:282
  36.2 2.2 %copy-start = (bf16[512,4096]{1,0:T(8,128)(2,1)S(1)}, bf16[512,4096]{1,0:T(8,128)(2,1)}, u32[]{:S(2)}) copy-start(bf16[512,4096]{1,0:T(8,128)(2,1)} %grad_ref.1) | copy-start | bytes 12582916
  38.4 1.1 %copy-start.3 = (bf16[448,544]{1,0:T(8,128)(2,1)S(1)}, bf16[448,544]{1,0:T(8,128)(2,1)}, u32[]{:S(2)}) copy-start(bf16[448,544]{1,0:T(8,128)(2,1)} %get-tuple-element.10.hidden_ref) | copy-start | bytes 1462276
  43.9 13.4 %collective-permute-start.8 = (bf16[2,448,128]{2,1,0:T(8,128)(2,1)S(1)}, bf16[2,448,128]{2,1,0:T(8,128)(2,1)S(1)}, u32[]{:S(2)}, u32[]{:S(2)}) collective-permute-start(bf16[2,448,128]{2,1,0:T(8,128)(2,1)S(1)} %shard_map.110), channel_id=1, source_target_pairs={{0,224},{32,0},{64,32},{96,64},{128,96},{160,128},{192,160},{224,1... | collective-permute-start | bytes 688136 | tf_op jit(solution)/shard_map/ppermute | solution.py:278
  46.9 14.4 %collective-permute-start.11 = (bf16[2,448,128]{2,1,0:T(8,128)(2,1)S(1)}, bf16[2,448,128]{2,1,0:T(8,128)(2,1)S(1)}, u32[]{:S(2)}, u32[]{:S(2)}) collective-permute-start(bf16[2,448,128]{2,1,0:T(8,128)(2,1)S(1)} %shard_map.113), channel_id=1, source_target_pairs={{0,224},{32,0},{64,32},{96,64},{128,96},{160,128},{192,160},{224,1... | collective-permute-start | bytes 688136 | tf_op jit(solution)/shard_map/ppermute | solution.py:278
  50.0 14.2 %collective-permute-start.1 = (bf16[2,448,128]{2,1,0:T(8,128)(2,1)S(1)}, bf16[2,448,128]{2,1,0:T(8,128)(2,1)S(1)}, u32[]{:S(2)}, u32[]{:S(2)}) collective-permute-start(bf16[2,448,128]{2,1,0:T(8,128)(2,1)S(1)} %shard_map.104), channel_id=1, source_target_pairs={{0,32},{32,64},{64,96},{96,128},{128,160},{160,192},{192,224},{224... | collective-permute-start | bytes 688136 | tf_op jit(solution)/shard_map/ppermute | solution.py:278
  53.9 14.0 %collective-permute-start.4 = (bf16[2,448,128]{2,1,0:T(8,128)(2,1)S(1)}, bf16[2,448,128]{2,1,0:T(8,128)(2,1)S(1)}, u32[]{:S(2)}, u32[]{:S(2)}) collective-permute-start(bf16[2,448,128]{2,1,0:T(8,128)(2,1)S(1)} %shard_map.107), channel_id=1, source_target_pairs={{0,32},{32,64},{64,96},{96,128},{128,160},{160,192},{192,224},{224... | collective-permute-start | bytes 688136 | tf_op jit(solution)/shard_map/ppermute | solution.py:278
  57.6 12.7 %collective-permute-start.9 = (bf16[2,448,128]{2,1,0:T(8,128)(2,1)S(1)}, bf16[2,448,128]{2,1,0:T(8,128)(2,1)S(1)}, u32[]{:S(2)}, u32[]{:S(2)}) collective-permute-start(bf16[2,448,128]{2,1,0:T(8,128)(2,1)S(1)} %shard_map.111), channel_id=1, source_target_pairs={{0,224},{32,0},{64,32},{96,64},{128,96},{160,128},{192,160},{224,1... | collective-permute-start | bytes 688136 | tf_op jit(solution)/shard_map/ppermute | solution.py:278
  61.7 14.0 %collective-permute-start.12 = (bf16[2,448,128]{2,1,0:T(8,128)(2,1)S(1)}, bf16[2,448,128]{2,1,0:T(8,128)(2,1)S(1)}, u32[]{:S(2)}, u32[]{:S(2)}) collective-permute-start(bf16[2,448,128]{2,1,0:T(8,128)(2,1)S(1)} %shard_map.114), channel_id=1, source_target_pairs={{0,224},{32,0},{64,32},{96,64},{128,96},{160,128},{192,160},{224,1... | collective-permute-start | bytes 688136 | tf_op jit(solution)/shard_map/ppermute | solution.py:278
  64.5 14.0 %collective-permute-start.2 = (bf16[2,448,128]{2,1,0:T(8,128)(2,1)S(1)}, bf16[2,448,128]{2,1,0:T(8,128)(2,1)S(1)}, u32[]{:S(2)}, u32[]{:S(2)}) collective-permute-start(bf16[2,448,128]{2,1,0:T(8,128)(2,1)S(1)} %shard_map.105), channel_id=1, source_target_pairs={{0,32},{32,64},{64,96},{96,128},{128,160},{160,192},{192,224},{224... | collective-permute-start | bytes 688136 | tf_op jit(solution)/shard_map/ppermute | solution.py:278
  68.2 14.0 %collective-permute-start.5 = (bf16[2,448,128]{2,1,0:T(8,128)(2,1)S(1)}, bf16[2,448,128]{2,1,0:T(8,128)(2,1)S(1)}, u32[]{:S(2)}, u32[]{:S(2)}) collective-permute-start(bf16[2,448,128]{2,1,0:T(8,128)(2,1)S(1)} %shard_map.108), channel_id=1, source_target_pairs={{0,32},{32,64},{64,96},{96,128},{128,160},{160,192},{192,224},{224... | collective-permute-start | bytes 688136 | tf_op jit(solution)/shard_map/ppermute | solution.py:278
  70.7 13.7 %collective-permute-start.10 = (bf16[2,448,128]{2,1,0:T(8,128)(2,1)S(1)}, bf16[2,448,128]{2,1,0:T(8,128)(2,1)S(1)}, u32[]{:S(2)}, u32[]{:S(2)}) collective-permute-start(bf16[2,448,128]{2,1,0:T(8,128)(2,1)S(1)} %shard_map.112), channel_id=1, source_target_pairs={{0,224},{32,0},{64,32},{96,64},{128,96},{160,128},{192,160},{224,1... | collective-permute-start | bytes 688136 | tf_op jit(solution)/shard_map/ppermute | solution.py:278
  76.0 8.5 %collective-permute-start.13 = (bf16[2,448,128]{2,1,0:T(8,128)(2,1)S(1)}, bf16[2,448,128]{2,1,0:T(8,128)(2,1)S(1)}, u32[]{:S(2)}, u32[]{:S(2)}) collective-permute-start(bf16[2,448,128]{2,1,0:T(8,128)(2,1)S(1)} %shard_map.115), channel_id=1, source_target_pairs={{0,224},{32,0},{64,32},{96,64},{128,96},{160,128},{192,160},{224,1... | collective-permute-start | bytes 688136 | tf_op jit(solution)/shard_map/ppermute | solution.py:278
  78.8 9.1 %collective-permute-start.3 = (bf16[2,448,128]{2,1,0:T(8,128)(2,1)S(1)}, bf16[2,448,128]{2,1,0:T(8,128)(2,1)S(1)}, u32[]{:S(2)}, u32[]{:S(2)}) collective-permute-start(bf16[2,448,128]{2,1,0:T(8,128)(2,1)S(1)} %shard_map.106), channel_id=1, source_target_pairs={{0,32},{32,64},{64,96},{96,128},{128,160},{160,192},{192,224},{224... | collective-permute-start | bytes 688136 | tf_op jit(solution)/shard_map/ppermute | solution.py:278
  82.5 9.1 %collective-permute-start.6 = (bf16[2,448,128]{2,1,0:T(8,128)(2,1)S(1)}, bf16[2,448,128]{2,1,0:T(8,128)(2,1)S(1)}, u32[]{:S(2)}, u32[]{:S(2)}) collective-permute-start(bf16[2,448,128]{2,1,0:T(8,128)(2,1)S(1)} %shard_map.109), channel_id=1, source_target_pairs={{0,32},{32,64},{64,96},{96,128},{128,160},{160,192},{192,224},{224... | collective-permute-start | bytes 688136 | tf_op jit(solution)/shard_map/ppermute | solution.py:278

commit v2 on v0

--- a/solution.py
+++ b/solution.py
@@ -46,11 +46,12 @@
             at = stop - start
             for z in range(outer):
                 message[z, at : at + orphans] = o_grad_refs[z][...]
-                piece = extra[:, min(start + z * cols, stop) : min(start + (z + 1) * cols, stop)]
+                left = start + z % (outer // 2) * cols
+                piece = extra[:, left : min(left + cols, stop)]
                 piece = piece.astype(jnp.bfloat16)
                 if piece.shape[1] < cols:
                     gap = jnp.zeros((orphans, cols - piece.shape[1]), jnp.bfloat16)
-                    piece = jnp.concatenate([piece, gap], axis=1) if piece.shape[1] else gap
+                    piece = jnp.concatenate([piece, gap], axis=1)
                 message[z, at + orphans :] = piece
 
     def column_block(height, z):
@@ -88,17 +89,46 @@
     )(order, place, gate, up, o_gate, o_up, *[grad] * outer, *[o_grad] * outer)
 
 
-def other_terms(order, place, names, hidden, grad, o_grad):
-    rows, _ = hidden.shape
+def write_terms(aways, order_ref, place, hidden_ref, grad_ref, o_grad_ref, weight, factor, ring_ref):
+    inner, outer = lax.axis_size("dp_1"), lax.axis_size("dp_0")
+    cols = ring_ref.shape[-1]
+    for turn, away in enumerate(aways):
+        to = lax.rem(place + away, inner)
+
+        def block(z):
+            at = pl.ds(pl.multiple_of(order_ref[z * inner + to] * cols, cols), cols)
+            own = grad_ref[:, at].astype(jnp.float32) * weight
+            extra = o_grad_ref[:, at].astype(jnp.float32) * factor
+            return jnp.concatenate([own.astype(jnp.bfloat16), extra.astype(jnp.bfloat16)], axis=0)
+
+        for first in range(0, outer, 2):
+            both = jnp.concatenate([block(first), block(first + 1)], axis=1)
+            term = jnp.dot(hidden_ref[...], both, preferred_element_type=jnp.float32)
+            for k in range(2):
+                ring_ref[turn, first + k] = term[:, k * cols : (k + 1) * cols]
+
+
+def terms_cost(shape, depth):
+    count, outer, rows, cols = shape
+    return pl.CostEstimate(
+        flops=2 * count * outer * rows * depth * cols,
+        bytes_accessed=2 * depth * count * outer * cols + 4 * count * outer * rows * cols,
+        transcendentals=0,
+    )
+
+
+def second_terms(aways, order, place, me, names, hidden, grad, o_grad):
+    rows, depth = hidden.shape
     own_rows, _ = grad.shape
     outer, inner = lax.axis_size("dp_0"), lax.axis_size("dp_1")
     replicas = outer * inner
     orphans = o_grad.shape[0]
     cols = grad.shape[1] // replicas
+    shape = (len(aways), outer, rows, cols)
 
     def kernel(
-        order_ref, place_ref, names_ref, hidden_ref, grad_ref, o_grad_ref,
-        ring_ref, weight_ref, load_ref, up_ref, down_ref,
+        order_ref, place_ref, me_ref, names_ref, hidden_ref, grad_ref, o_grad_ref,
+        ring_ref, weight_ref, load_ref, *factor_refs,
     ):
         names = names_ref[...].T
         lanes = lax.broadcasted_iota(jnp.int32, (orphans, replicas), 1)
@@ -108,9 +138,9 @@
             taken = taken + (names[:, holder : holder + 1] == marks).astype(jnp.float32)
         taken = jnp.sum(taken, axis=0, keepdims=True)
         weights = 1.0 / (own_rows + taken)
-        line = place_ref[1] - place_ref[0]
+        line = me_ref[0] - place_ref[0]
         holders = [
-            place_ref[1],
+            me_ref[0],
             line + lax.rem(place_ref[0] + inner - 1, inner),
             line + lax.rem(place_ref[0] + 1, inner),
         ]
@@ -119,57 +149,57 @@
             return jnp.sum(jnp.where(lanes[:1] == holder, row, 0.0), axis=1, keepdims=True)
 
         load_ref[...] = entry(taken, holders[0]) / orphans
-        factors = []
         for k, holder in enumerate(holders):
             weight_ref[k : k + 1] = jnp.broadcast_to(entry(weights, holder), (1, cols))
             column = jnp.sum(jnp.where(lanes == holder, names, 0.0), axis=1, keepdims=True)
-            factors.append(
-                jnp.sum(jnp.where(column == marks, weights, 0.0), axis=1, keepdims=True)
-            )
-        up_ref[...] = jnp.broadcast_to(factors[1], up_ref.shape)
-        down_ref[...] = jnp.broadcast_to(factors[2], down_ref.shape)
-        own_weight = weight_ref[:1]
-
-        for turn in range(inner - 1):
-            away = turn + 1 + (turn + 1) // (inner // 2)
-            to = lax.rem(place_ref[0] + away, inner)
-
-            def block(z):
-                at = pl.ds(pl.multiple_of(order_ref[z * inner + to] * cols, cols), cols)
-                own = grad_ref[:, at].astype(jnp.float32) * own_weight
-                extra = o_grad_ref[:, at].astype(jnp.float32) * factors[0]
-                return jnp.concatenate([own.astype(jnp.bfloat16), extra.astype(jnp.bfloat16)], axis=0)
-
-            for first in range(0, outer, 2):
-                both = jnp.concatenate([block(first), block(first + 1)], axis=1)
-                term = jnp.dot(hidden_ref[...], both, preferred_element_type=jnp.float32)
-                for k in range(2):
-                    ring_ref[turn, first + k] = term[:, k * cols : (k + 1) * cols]
-
-    return pl.pallas_call(
-        kernel,
-        name="other_terms",
+            factor = jnp.sum(jnp.where(column == marks, weights, 0.0), axis=1, keepdims=True)
+            factor_refs[k][...] = jnp.broadcast_to(factor, (orphans, cols))
+        write_terms(
+            aways, order_ref, place_ref[0], hidden_ref, grad_ref, o_grad_ref,
+            weight_ref[:1], factor_refs[0][...], ring_ref,
+        )
+
+    return pl.pallas_call(
+        kernel,
+        name="second_terms",
         out_shape=(
-            jax.ShapeDtypeStruct((inner - 1, outer, rows, cols), jnp.float32),
+            jax.ShapeDtypeStruct(shape, jnp.float32),
             jax.ShapeDtypeStruct((3, cols), jnp.float32),
             jax.ShapeDtypeStruct((1, 1), jnp.float32),
-            jax.ShapeDtypeStruct((orphans, cols), jnp.float32),
-            jax.ShapeDtypeStruct((orphans, cols), jnp.float32),
-        ),
-        in_specs=[SMEM] * 2 + [VMEM] * 4,
-        out_specs=(VMEM,) * 5,
-        compiler_params=room(20),
-        cost_estimate=pl.CostEstimate(
-            flops=2 * rows * hidden.shape[1] * grad.shape[1],
-            bytes_accessed=2 * hidden.shape[1] * grad.shape[1] + 4 * rows * grad.shape[1],
-            transcendentals=0,
-        ),
-    )(order, place, names, hidden, grad, o_grad)
-
-
-def ring_sum(away, ring, received, first=None):
-    inner, outer, rows, cols = ring.shape[0] + 1, *ring.shape[1:]
-    at = (away - 1 - away // (inner // 2)) % inner if away else inner - 2
+            *[jax.ShapeDtypeStruct((orphans, cols), jnp.float32)] * 3,
+        ),
+        in_specs=[SMEM] * 3 + [VMEM] * 4,
+        out_specs=(VMEM,) * 6,
+        compiler_params=room(16),
+        cost_estimate=terms_cost(shape, depth),
+    )(order, place, me, names, hidden, grad, o_grad)
+
+
+def other_terms(aways, order, place, weight, factor, hidden, grad, o_grad):
+    rows, depth = hidden.shape
+    shape = (len(aways), lax.axis_size("dp_0"), rows, weight.shape[1])
+
+    def kernel(
+        order_ref, place_ref, weight_ref, factor_ref, hidden_ref, grad_ref, o_grad_ref, ring_ref
+    ):
+        write_terms(
+            aways, order_ref, place_ref[0], hidden_ref, grad_ref, o_grad_ref,
+            weight_ref[:1], factor_ref[...], ring_ref,
+        )
+
+    return pl.pallas_call(
+        kernel,
+        name="other_terms",
+        out_shape=jax.ShapeDtypeStruct(shape, jnp.float32),
+        in_specs=[SMEM] * 2 + [VMEM] * 5,
+        out_specs=VMEM,
+        compiler_params=room(16),
+        cost_estimate=terms_cost(shape, depth),
+    )(order, place, weight, factor, hidden, grad, o_grad)
+
+
+def ring_sum(at, ring, received, first=None):
+    outer, rows, cols = ring.shape[1:]
     operands = [*received, *([] if first is None else [first[0], first[2]])]
 
     def kernel(ring_ref, *refs):
@@ -179,10 +209,10 @@
         if first is not None:
             message, weight_ref, factor_ref = came
             orphans = factor_ref.shape[0]
-            count = message.shape[1] - 2 * orphans
-            pieces = [message[z, count + orphans :] for z in range(-(-count // cols))]
+            own = message.shape[1] - 2 * orphans
+            pieces = [message[z, own + orphans :] for z in range(outer // 2)]
             theirs = jnp.concatenate(pieces, axis=1).astype(jnp.float32).T
-            theirs = theirs[:count].astype(jnp.bfloat16)
+            theirs = theirs[:own].astype(jnp.bfloat16)
         copy.wait()
         for z in range(outer):
             if first is None:
@@ -192,14 +222,14 @@
                 out_ref[z] = total.astype(jnp.bfloat16)
                 continue
             _, row, _, start = first
-            scaled = message[z, count : count + orphans].astype(jnp.float32) * factor_ref[...]
-            part = message[z, :count].astype(jnp.float32) * weight_ref[row : row + 1]
+            scaled = message[z, own : own + orphans].astype(jnp.float32) * factor_ref[...]
+            part = message[z, :own].astype(jnp.float32) * weight_ref[row : row + 1]
             part = part + jnp.dot(
                 theirs, scaled.astype(jnp.bfloat16), preferred_element_type=jnp.float32
             )
             out_ref[z] = own_ref[z].astype(jnp.bfloat16)
-            part = own_ref[z, start : start + count] + part
-            out_ref[z, start : start + count] = part.astype(jnp.bfloat16)
+            part = own_ref[z, start : start + own] + part
+            out_ref[z, start : start + own] = part.astype(jnp.bfloat16)
 
     return pl.pallas_call(
         kernel,
@@ -258,15 +288,16 @@
     replicas = lax.axis_size(DP)
     inner = lax.axis_size("dp_1")
     me = lax.axis_index(DP).astype(jnp.int32)
-    place = jnp.stack([lax.axis_index("dp_1").astype(jnp.int32), me])
+    line = lax.axis_index("dp_1").astype(jnp.int32).reshape(1)
+    me = me.reshape(1)
     orphans = orphan_grad.shape[0]
-    live = jnp.arange(orphans, dtype=jnp.int32) < orphan_len[0]
-    names = jnp.where(live, orphan_dest[:, 0], -1).astype(jnp.float32)
-    names = jnp.broadcast_to(names[None, None], (replicas, 1, orphans))
+    live = lax.broadcasted_iota(jnp.int32, (replicas, 1, orphans), 2) < orphan_len[0]
+    names = jnp.broadcast_to(orphan_dest[:, 0][None, None], live.shape)
+    names = jnp.where(live, names, -1).astype(jnp.float32)
     names = exchanged(names, DP)
     hidden, up, down = first_message(
         loop_order,
-        place,
+        line,
         local_gate,
         local_up,
         orphan_gate.T,
@@ -275,15 +306,30 @@
         orphan_grad,
     )
     up, down = shifted(up, 1), shifted(down, -1)
-    ring, weight, load, up_factor, down_factor = other_terms(
-        loop_order, place, names.reshape(replicas, orphans), hidden, local_grad, orphan_grad
+    far = inner // 2
+    near_by = [*range(1, far - 1), *range(far + 2, inner), 0]
+    second, weight, load, factor, up_factor, down_factor = second_terms(
+        (far - 1, far + 1),
+        loop_order,
+        line,
+        me,
+        names.reshape(replicas, orphans),
+        hidden,
+        local_grad,
+        orphan_grad,
     )
     ups, downs = (weight, 1, up_factor, 0), (weight, 2, down_factor, UP_ROWS)
-    for away in range(inner // 2 - 1, 0, -1):
-        up = shifted(ring_sum(away, ring, [up], ups), 1)
-        down = shifted(ring_sum(inner - away, ring, [down], downs), -1)
-        ups = downs = None
-    near = ring_sum(0, ring, [up, down])
+    up = ring_sum(0, second, [up], ups)
+    up = shifted(up, 1)
+    down = ring_sum(1, second, [down], downs)
+    down = shifted(down, -1)
+    ring = other_terms(near_by, loop_order, line, weight, factor, hidden, local_grad, orphan_grad)
+    for away in range(far - 2, 0, -1):
+        up = ring_sum(near_by.index(away), ring, [up])
+        up = shifted(up, 1)
+        down = ring_sum(near_by.index(inner - away), ring, [down])
+        down = shifted(down, -1)
+    near = ring_sum(near_by.index(0), ring, [up, down])
     return total_of(exchanged(near, "dp_0")), load.reshape(1)
 
 

time: 97 us -> 97.4 us (level)
  blocking collectives: 34.2 us -> 11.8 us
  starting transfers between devices: 23.8 us -> 38.3 us
  waiting for transfers between devices: 22.1 us -> 29.4 us
  Pallas kernels: 10.9 us -> 11.9 us
    all_to_all x2 -> x1, blocking collectives: 34.2 us -> 11.8 us  [exchanged(): return lax.all_to_all(array, axis, split_axis=0, concat_axis=0, tiled=True)]
    all_to_all x0 -> x1, starting transfers between devices: none -> 14.3 us  [exchanged(): return lax.all_to_all(array, axis, split_axis=0, concat_axis=0, tiled=True)]
    all_to_all x0 -> x1, waiting for transfers between devices: none -> 8.91 us  [exchanged(): return lax.all_to_all(array, axis, split_axis=0, concat_axis=0, tiled=True)]
    ppermute x8, waiting for transfers between devices: 22.1 us -> 20.5 us  [shifted(): lax.ppermute(array, 'dp_1', [(i, (i + by) % size) for i in range(size)])]
    pallas_call x1 -> x2, Pallas kernels: 3.86 us -> 4.74 us  [the longest x1 2.6 us: other_terms(): pl.pallas_call(kernel, name='other_terms', out_shape=jax.ShapeDtypeStruct...]
    unnamed x12 -> x10, local copies, waits for them, and re-layouts: 3.26 us -> 3.26 us
  transfers between devices with their start and end apart: 8 -> 9, of which waited for: 6 -> 7; matrix products, arithmetic and copies ran while one was open for 0% -> 1% of each run, Pallas kernels for 6% -> 7%
where the time goes in v2:
time: 97.4 us; the launch traced here: 96.8 us
  starting transfers between devices  38.3 us (39%)
  waiting for transfers between devices  29.4 us (30%)
  Pallas kernels  11.9 us (12%)
  blocking collectives  11.8 us (12%)
  local copies, waits for them, and re-layouts  3.26 us (3%)
  between operations  1.48 us (2%)
    ppermute x8, starting transfers between devices, shifted(): lax.ppermute(array, 'dp_1', [(i, (i + by) % size) for i in range(size)])  24 us
    ppermute x8, waiting for transfers between devices, shifted(): lax.ppermute(array, 'dp_1', [(i, (i + by) % size) for i in range(size)])  20.5 us
    all_to_all x1, starting transfers between devices, exchanged(): return lax.all_to_all(array, axis, split_axis=0, concat_axis=0, tiled=True)  14.3 us
    all_to_all x1, blocking collectives, exchanged(): return lax.all_to_all(array, axis, split_axis=0, concat_axis=0, tiled=True)  11.8 us
    all_to_all x1, waiting for transfers between devices, exchanged(): return lax.all_to_all(array, axis, split_axis=0, concat_axis=0, tiled=True)  8.91 us
    pallas_call x1, Pallas kernels, first_message(): pl.pallas_call(kernel, name='first_message', out_shape=[jax.ShapeDtypeStr...  3.64 us
    unnamed x10, local copies, waits for them, and re-layouts  3.26 us
    pallas_call x7, Pallas kernels, ring_sum(): pl.pallas_call(kernel, out_shape=jax.ShapeDtypeStruct((outer, rows, cols)...  2.8 us
  transfers between devices with their start and end apart: 9, of which 7 were waited for; matrix products, arithmetic and copies ran while one was open for 1% of the time, Pallas kernels for 7%

profile of v2, /device:TPU:64, one launch (start us, length us, event | category | flops | bytes accessed | tf_op | source)
XLA Modules:
  0.0 96.8 jit_solution(8446948144729467782)
XLA Ops:
  0.6 0.0 copy-start.4
  0.6 0.0 copy-start.1
  0.7 0.0 copy-start.3
  0.7 3.6 %first_message.1 = (bf16[448,544]{1,0:T(8,128)(2,1)}, bf16[4,320,128]{2,1,0:T(8,128)(2,1)}, bf16[4,256,128]{2,1,0:T(8,128)(2,1)}) custom-call(s32[32]{0:T(128)} %order_ref.5, s32[1]{0:T(128)} %bitcast.place_ref, bf16[448,512]{1,0:T(8,128)(2,1)} %gate_ref.1, bf16[448,512]{1,0:T(8,128)(2,1)} %up_ref.1, bf16[32,448]{1,0:T(8,128)(2,1)} %bitcast.10, ...), custom_call_target="tpu_custom_call" | custom-call | flops 234881024 | bytes 1835008 | tf_op jit(solution)/shard_map/first_message/pallas_call | solution.py:71
  4.3 5.4 %collective-permute-start.4 = (bf16[4,256,128]{2,1,0:T(8,128)(2,1)}, bf16[4,256,128]{2,1,0:T(8,128)(2,1)S(1)}, u32[]{:S(2)}, u32[]{:S(2)}) collective-permute-start(bf16[4,256,128]{2,1,0:T(8,128)(2,1)} %get-tuple-element.17), channel_id=1, source_target_pairs={{0,224},{32,0},{64,32},{96,64},{128,96},{160,128},{192,160},{224,1... | collective-permute-start | bytes 786440 | tf_op jit(solution)/shard_map/ppermute | solution.py:270
  9.7 1.9 %collective-permute-start = (bf16[4,320,128]{2,1,0:T(8,128)(2,1)}, bf16[4,320,128]{2,1,0:T(8,128)(2,1)S(1)}, u32[]{:S(2)}, u32[]{:S(2)}) collective-permute-start(bf16[4,320,128]{2,1,0:T(8,128)(2,1)} %get-tuple-element.15), channel_id=1, source_target_pairs={{0,32},{32,64},{64,96},{96,128},{128,160},{160,192},{192,224},{224... | collective-permute-start | bytes 983048 | tf_op jit(solution)/shard_map/ppermute | solution.py:270
  12.3 0.0 copy-done.4
  12.3 0.6 fusion
  12.9 14.3 %all-to-all-start = ((f32[32,1,32]{2,1,0:T(1,128)}), f32[32,1,32]{2,1,0:T(1,128)S(1)}, u32[]{:S(2)}, u32[]{:S(2)}) async-start(f32[32,1,32]{2,1,0:T(1,128)} %fusion), calls=%async_computation | async-start | bytes 32768 | tf_op jit(solution)/shard_map/all_to_all | solution.py:274
  27.3 8.9 %all-to-all-done = f32[32,1,32]{2,1,0:T(1,128)S(1)} async-done(((f32[32,1,32]{2,1,0:T(1,128)}), f32[32,1,32]{2,1,0:T(1,128)S(1)}, u32[]{:S(2)}, u32[]{:S(2)}) %all-to-all-start) | async-done | bytes 4128 | tf_op jit(solution)/shard_map/all_to_all | solution.py:274
  36.2 0.0 copy-done.1
  36.2 0.0 copy-done.3
  36.2 0.0 copy-start
  36.2 2.2 %copy-done = bf16[512,4096]{1,0:T(8,128)(2,1)S(1)} copy-done((bf16[512,4096]{1,0:T(8,128)(2,1)S(1)}, bf16[512,4096]{1,0:T(8,128)(2,1)}, u32[]{:S(2)}) %copy-start) | copy-done | bytes 4194328
  38.4 0.0 copy-start.2
  38.4 1.1 %copy-done.2 = bf16[448,544]{1,0:T(8,128)(2,1)S(1)} copy-done((bf16[448,544]{1,0:T(8,128)(2,1)S(1)}, bf16[448,544]{1,0:T(8,128)(2,1)}, u32[]{:S(2)}) %copy-start.2) | copy-done | bytes 487448
  39.4 2.1 %second_terms.1 = (f32[2,4,448,128]{3,2,1,0:T(8,128)S(1)}, f32[3,128]{1,0:T(4,128)S(1)}, f32[1,1]{1,0:T(1,128)}, f32[32,128]{1,0:T(8,128)S(1)}, f32[32,128]{1,0:T(8,128)S(1)}, /*index=5*/f32[32,128]{1,0:T(8,128)S(1)}) custom-call(s32[32]{0:T(128)S(1)} %copy-done.3, s32[1]{0:T(128)} %bitcast.place_ref, s32[1]{0:T(128)} %bitcast.1.me_ref, ...), custom_call_target="tpu_custom_call" | custom-call | flops 499122176 | bytes 2949120 | tf_op jit(solution)/shard_map/second_terms/pallas_call | solution.py:162
  41.6 0.0 collective-permute-done.4.refs_0_
  41.6 0.5 shard_map.107
  42.1 2.5 %collective-permute-start.5 = (bf16[4,448,128]{2,1,0:T(8,128)(2,1)S(1)}, bf16[4,448,128]{2,1,0:T(8,128)(2,1)S(1)}, u32[]{:S(2)}, u32[]{:S(2)}) collective-permute-start(bf16[4,448,128]{2,1,0:T(8,128)(2,1)S(1)} %shard_map.107), channel_id=1, source_target_pairs={{0,224},{32,0},{64,32},{96,64},{128,96},{160,128},{192,160},{224,1... | collective-permute-start | bytes 1376264 | tf_op jit(solution)/shard_map/ppermute | solution.py:270
  44.6 0.0 collective-permute-done.refs_0_
  44.6 0.6 shard_map.104
  45.2 3.4 %collective-permute-start.1 = (bf16[4,448,128]{2,1,0:T(8,128)(2,1)S(1)}, bf16[4,448,128]{2,1,0:T(8,128)(2,1)S(1)}, u32[]{:S(2)}, u32[]{:S(2)}) collective-permute-start(bf16[4,448,128]{2,1,0:T(8,128)(2,1)S(1)} %shard_map.104), channel_id=1, source_target_pairs={{0,32},{32,64},{64,96},{96,128},{128,160},{160,192},{192,224},{224... | collective-permute-start | bytes 1376264 | tf_op jit(solution)/shard_map/ppermute | solution.py:270
  48.6 2.6 %other_terms.1.ring_ref = f32[5,4,448,128]{3,2,1,0:T(8,128)S(1)} custom-call(s32[32]{0:T(128)S(1)} %copy-done.3, s32[1]{0:T(128)} %bitcast.place_ref, f32[3,128]{1,0:T(4,128)S(1)} %get-tuple-element.12.weight_ref.refs_1_, f32[32,128]{1,0:T(8,128)S(1)} %get-tuple-element.13.factor_ref, bf16[448,544]{1,0:T(8,128)(2,1)S(1)} %copy-done.2, ...), custom_call_target="tpu_custom_call" | custom-call | flops 1247805440 | bytes 7372800 | tf_op jit(solution)/shard_map/other_terms/pallas_call | solution.py:190
  51.2 3.3 %collective-permute-done.5.refs_0_ = bf16[4,448,128]{2,1,0:T(8,128)(2,1)S(1)} collective-permute-done((bf16[4,448,128]{2,1,0:T(8,128)(2,1)S(1)}, bf16[4,448,128]{2,1,0:T(8,128)(2,1)S(1)}, u32[]{:S(2)}, u32[]{:S(2)}) %collective-permute-start.5) | collective-permute-done | bytes 458784 | tf_op jit(solution)/shard_map/ppermute | solution.py:270
  54.5 0.3 shard_map.108
  54.8 2.5 %collective-permute-start.6 = (bf16[4,448,128]{2,1,0:T(8,128)(2,1)S(1)}, bf16[4,448,128]{2,1,0:T(8,128)(2,1)S(1)}, u32[]{:S(2)}, u32[]{:S(2)}) collective-permute-start(bf16[4,448,128]{2,1,0:T(8,128)(2,1)S(1)} %shard_map.108), channel_id=1, source_target_pairs={{0,224},{32,0},{64,32},{96,64},{128,96},{160,128},{192,160},{224,1... | collective-permute-start | bytes 1376264 | tf_op jit(solution)/shard_map/ppermute | solution.py:270
  57.3 0.5 collective-permute-done.1.refs_0_
  57.8 0.3 shard_map.105
  58.2 3.1 %collective-permute-start.2 = (bf16[4,448,128]{2,1,0:T(8,128)(2,1)S(1)}, bf16[4,448,128]{2,1,0:T(8,128)(2,1)S(1)}, u32[]{:S(2)}, u32[]{:S(2)}) collective-permute-start(bf16[4,448,128]{2,1,0:T(8,128)(2,1)S(1)} %shard_map.105), channel_id=1, source_target_pairs={{0,32},{32,64},{64,96},{96,128},{128,160},{160,192},{192,224},{224... | collective-permute-start | bytes 1376264 | tf_op jit(solution)/shard_map/ppermute | solution.py:270
  61.3 6.8 %collective-permute-done.6.refs_0_ = bf16[4,448,128]{2,1,0:T(8,128)(2,1)S(1)} collective-permute-done((bf16[4,448,128]{2,1,0:T(8,128)(2,1)S(1)}, bf16[4,448,128]{2,1,0:T(8,128)(2,1)S(1)}, u32[]{:S(2)}, u32[]{:S(2)}) %collective-permute-start.6) | collective-permute-done | bytes 458784 | tf_op jit(solution)/shard_map/ppermute | solution.py:270
  68.1 0.3 shard_map.109
  68.4 2.8 %collective-permute-start.7 = (bf16[4,448,128]{2,1,0:T(8,128)(2,1)S(1)}, bf16[4,448,128]{2,1,0:T(8,128)(2,1)S(1)}, u32[]{:S(2)}, u32[]{:S(2)}) collective-permute-start(bf16[4,448,128]{2,1,0:T(8,128)(2,1)S(1)} %shard_map.109), channel_id=1, source_target_pairs={{0,224},{32,0},{64,32},{96,64},{128,96},{160,128},{192,160},{224,1... | collective-permute-start | bytes 1376264 | tf_op jit(solution)/shard_map/ppermute | solution.py:270
  71.2 0.8 collective-permute-done.2.refs_0_
  72.0 0.3 shard_map.106
  72.3 2.5 %collective-permute-start.3 = (bf16[4,448,128]{2,1,0:T(8,128)(2,1)S(1)}, bf16[4,448,128]{2,1,0:T(8,128)(2,1)S(1)}, u32[]{:S(2)}, u32[]{:S(2)}) collective-permute-start(bf16[4,448,128]{2,1,0:T(8,128)(2,1)S(1)} %shard_map.106), channel_id=1, source_target_pairs={{0,32},{32,64},{64,96},{96,128},{128,160},{160,192},{192,224},{224... | collective-permute-start | bytes 1376264 | tf_op jit(solution)/shard_map/ppermute | solution.py:270
  74.8 4.0 %collective-permute-done.7.refs_1_ = bf16[4,448,128]{2,1,0:T(8,128)(2,1)S(1)} collective-permute-done((bf16[4,448,128]{2,1,0:T(8,128)(2,1)S(1)}, bf16[4,448,128]{2,1,0:T(8,128)(2,1)S(1)}, u32[]{:S(2)}, u32[]{:S(2)}) %collective-permute-start.7) | collective-permute-done | bytes 458784 | tf_op jit(solution)/shard_map/ppermute | solution.py:270
  78.8 5.1 %collective-permute-done.3.refs_0_ = bf16[4,448,128]{2,1,0:T(8,128)(2,1)S(1)} collective-permute-done((bf16[4,448,128]{2,1,0:T(8,128)(2,1)S(1)}, bf16[4,448,128]{2,1,0:T(8,128)(2,1)S(1)}, u32[]{:S(2)}, u32[]{:S(2)}) %collective-permute-start.3) | collective-permute-done | bytes 458784 | tf_op jit(solution)/shard_map/ppermute | solution.py:270
  83.9 0.4 shard_map.110
  84.3 11.8 %all_to_all.10.near_ref = bf16[4,448,128]{2,1,0:T(8,128)(2,1)S(1)} all-to-all(bf16[4,448,128]{2,1,0:T(8,128)(2,1)S(1)} %shard_map.110), channel_id=1, replica_groups=mesh['dp_0'=4,'dp_1'=8,'tensor'=32] {'dp_0'}, dimensions={0} | all-to-all | bytes 917504 | tf_op jit(solution)/shard_map/all_to_all | solution.py:274
  96.1 0.7 total_of.1
  (1 shorter events, 0.0 us)
Async XLA Ops:
  0.6 11.6 %copy-start.4 = (s32[32,1]{0,1:T(1,128)S(1)}, s32[32,1]{0,1:T(1,128)}, u32[]{:S(2)}) copy-start(s32[32,1]{0,1:T(1,128)} %param.16) | copy-start | bytes 388
  0.6 35.5 %copy-start.1 = (bf16[32,4096]{1,0:T(8,128)(2,1)S(1)}, bf16[32,4096]{1,0:T(8,128)(2,1)}, u32[]{:S(2)}) copy-start(bf16[32,4096]{1,0:T(8,128)(2,1)} %o_grad_ref.3) | copy-start | bytes 786436
  0.7 35.5 %copy-start.3 = (s32[32]{0:T(128)S(1)}, s32[32]{0:T(128)}, u32[]{:S(2)}) copy-start(s32[32]{0:T(128)} %order_ref.5) | copy-start | bytes 388
  4.3 37.3 %collective-permute-start.4 = (bf16[4,256,128]{2,1,0:T(8,128)(2,1)}, bf16[4,256,128]{2,1,0:T(8,128)(2,1)S(1)}, u32[]{:S(2)}, u32[]{:S(2)}) collective-permute-start(bf16[4,256,128]{2,1,0:T(8,128)(2,1)} %get-tuple-element.17), channel_id=1, source_target_pairs={{0,224},{32,0},{64,32},{96,64},{128,96},{160,128},{192,160},{224,1... | collective-permute-start | bytes 786440 | tf_op jit(solution)/shard_map/ppermute | solution.py:270
  9.7 34.9 %collective-permute-start = (bf16[4,320,128]{2,1,0:T(8,128)(2,1)}, bf16[4,320,128]{2,1,0:T(8,128)(2,1)S(1)}, u32[]{:S(2)}, u32[]{:S(2)}) collective-permute-start(bf16[4,320,128]{2,1,0:T(8,128)(2,1)} %get-tuple-element.15), channel_id=1, source_target_pairs={{0,32},{32,64},{64,96},{96,128},{128,160},{160,192},{192,224},{224... | collective-permute-start | bytes 983048 | tf_op jit(solution)/shard_map/ppermute | solution.py:270
  12.9 23.3 %all-to-all-start = ((f32[32,1,32]{2,1,0:T(1,128)}), f32[32,1,32]{2,1,0:T(1,128)S(1)}, u32[]{:S(2)}, u32[]{:S(2)}) async-start(f32[32,1,32]{2,1,0:T(1,128)} %fusion), calls=%async_computation | async-start | bytes 32768 | tf_op jit(solution)/shard_map/all_to_all | solution.py:274
  36.2 2.2 %copy-start = (bf16[512,4096]{1,0:T(8,128)(2,1)S(1)}, bf16[512,4096]{1,0:T(8,128)(2,1)}, u32[]{:S(2)}) copy-start(bf16[512,4096]{1,0:T(8,128)(2,1)} %grad_ref.3) | copy-start | bytes 12582916
  38.4 1.1 %copy-start.2 = (bf16[448,544]{1,0:T(8,128)(2,1)S(1)}, bf16[448,544]{1,0:T(8,128)(2,1)}, u32[]{:S(2)}) copy-start(bf16[448,544]{1,0:T(8,128)(2,1)} %get-tuple-element.11.hidden_ref) | copy-start | bytes 1462276
  42.1 12.4 %collective-permute-start.5 = (bf16[4,448,128]{2,1,0:T(8,128)(2,1)S(1)}, bf16[4,448,128]{2,1,0:T(8,128)(2,1)S(1)}, u32[]{:S(2)}, u32[]{:S(2)}) collective-permute-start(bf16[4,448,128]{2,1,0:T(8,128)(2,1)S(1)} %shard_map.107), channel_id=1, source_target_pairs={{0,224},{32,0},{64,32},{96,64},{128,96},{160,128},{192,160},{224,1... | collective-permute-start | bytes 1376264 | tf_op jit(solution)/shard_map/ppermute | solution.py:270
  45.2 12.6 %collective-permute-start.1 = (bf16[4,448,128]{2,1,0:T(8,128)(2,1)S(1)}, bf16[4,448,128]{2,1,0:T(8,128)(2,1)S(1)}, u32[]{:S(2)}, u32[]{:S(2)}) collective-permute-start(bf16[4,448,128]{2,1,0:T(8,128)(2,1)S(1)} %shard_map.104), channel_id=1, source_target_pairs={{0,32},{32,64},{64,96},{96,128},{128,160},{160,192},{192,224},{224... | collective-permute-start | bytes 1376264 | tf_op jit(solution)/shard_map/ppermute | solution.py:270
  54.8 13.2 %collective-permute-start.6 = (bf16[4,448,128]{2,1,0:T(8,128)(2,1)S(1)}, bf16[4,448,128]{2,1,0:T(8,128)(2,1)S(1)}, u32[]{:S(2)}, u32[]{:S(2)}) collective-permute-start(bf16[4,448,128]{2,1,0:T(8,128)(2,1)S(1)} %shard_map.108), channel_id=1, source_target_pairs={{0,224},{32,0},{64,32},{96,64},{128,96},{160,128},{192,160},{224,1... | collective-permute-start | bytes 1376264 | tf_op jit(solution)/shard_map/ppermute | solution.py:270
  58.2 13.8 %collective-permute-start.2 = (bf16[4,448,128]{2,1,0:T(8,128)(2,1)S(1)}, bf16[4,448,128]{2,1,0:T(8,128)(2,1)S(1)}, u32[]{:S(2)}, u32[]{:S(2)}) collective-permute-start(bf16[4,448,128]{2,1,0:T(8,128)(2,1)S(1)} %shard_map.105), channel_id=1, source_target_pairs={{0,32},{32,64},{64,96},{96,128},{128,160},{160,192},{192,224},{224... | collective-permute-start | bytes 1376264 | tf_op jit(solution)/shard_map/ppermute | solution.py:270
  68.4 10.4 %collective-permute-start.7 = (bf16[4,448,128]{2,1,0:T(8,128)(2,1)S(1)}, bf16[4,448,128]{2,1,0:T(8,128)(2,1)S(1)}, u32[]{:S(2)}, u32[]{:S(2)}) collective-permute-start(bf16[4,448,128]{2,1,0:T(8,128)(2,1)S(1)} %shard_map.109), channel_id=1, source_target_pairs={{0,224},{32,0},{64,32},{96,64},{128,96},{160,128},{192,160},{224,1... | collective-permute-start | bytes 1376264 | tf_op jit(solution)/shard_map/ppermute | solution.py:270
  72.3 11.6 %collective-permute-start.3 = (bf16[4,448,128]{2,1,0:T(8,128)(2,1)S(1)}, bf16[4,448,128]{2,1,0:T(8,128)(2,1)S(1)}, u32[]{:S(2)}, u32[]{:S(2)}) collective-permute-start(bf16[4,448,128]{2,1,0:T(8,128)(2,1)S(1)} %shard_map.106), channel_id=1, source_target_pairs={{0,32},{32,64},{64,96},{96,128},{128,160},{160,192},{192,224},{224... | collective-permute-start | bytes 1376264 | tf_op jit(solution)/shard_map/ppermute | solution.py:270

commit v3 on v2

--- a/solution.py
+++ b/solution.py
@@ -89,7 +89,7 @@
     )(order, place, gate, up, o_gate, o_up, *[grad] * outer, *[o_grad] * outer)
 
 
-def write_terms(aways, order_ref, place, hidden_ref, grad_ref, o_grad_ref, weight, factor, ring_ref):
+def write_terms(aways, order_ref, place, hidden_ref, own_at, o_grad_ref, weight, factor, ring_ref):
     inner, outer = lax.axis_size("dp_1"), lax.axis_size("dp_0")
     cols = ring_ref.shape[-1]
     for turn, away in enumerate(aways):
@@ -97,7 +97,7 @@
 
         def block(z):
             at = pl.ds(pl.multiple_of(order_ref[z * inner + to] * cols, cols), cols)
-            own = grad_ref[:, at].astype(jnp.float32) * weight
+            own = own_at(turn, z, at).astype(jnp.float32) * weight
             extra = o_grad_ref[:, at].astype(jnp.float32) * factor
             return jnp.concatenate([own.astype(jnp.bfloat16), extra.astype(jnp.bfloat16)], axis=0)
 
@@ -125,11 +125,21 @@
     orphans = o_grad.shape[0]
     cols = grad.shape[1] // replicas
     shape = (len(aways), outer, rows, cols)
+    blocks = len(aways) * outer
+
+    def column_block(away, z):
+        def at(turn, order_ref, place_ref, me_ref):
+            return 0, order_ref[z * inner + lax.rem(place_ref[0] + away, inner)]
+
+        return pl.BlockSpec((own_rows, cols), at)
+
+    def whole(array):
+        return pl.BlockSpec(array.shape, lambda turn, *_: (0,) * len(array.shape))
 
     def kernel(
-        order_ref, place_ref, me_ref, names_ref, hidden_ref, grad_ref, o_grad_ref,
-        ring_ref, weight_ref, load_ref, *factor_refs,
+        order_ref, place_ref, me_ref, names_ref, hidden_ref, o_grad_ref, *refs
     ):
+        grad_refs, (ring_ref, weight_ref, load_ref, *factor_refs) = refs[:blocks], refs[blocks:]
         names = names_ref[...].T
         lanes = lax.broadcasted_iota(jnp.int32, (orphans, replicas), 1)
         marks = lanes.astype(jnp.float32)
@@ -155,24 +165,31 @@
             factor = jnp.sum(jnp.where(column == marks, weights, 0.0), axis=1, keepdims=True)
             factor_refs[k][...] = jnp.broadcast_to(factor, (orphans, cols))
         write_terms(
-            aways, order_ref, place_ref[0], hidden_ref, grad_ref, o_grad_ref,
+            aways, order_ref, place_ref[0], hidden_ref,
+            lambda turn, z, _: grad_refs[turn * outer + z][...], o_grad_ref,
             weight_ref[:1], factor_refs[0][...], ring_ref,
         )
 
+    out_shape = (
+        jax.ShapeDtypeStruct(shape, jnp.float32),
+        jax.ShapeDtypeStruct((3, cols), jnp.float32),
+        jax.ShapeDtypeStruct((1, 1), jnp.float32),
+        *[jax.ShapeDtypeStruct((orphans, cols), jnp.float32)] * 3,
+    )
     return pl.pallas_call(
         kernel,
         name="second_terms",
-        out_shape=(
-            jax.ShapeDtypeStruct(shape, jnp.float32),
-            jax.ShapeDtypeStruct((3, cols), jnp.float32),
-            jax.ShapeDtypeStruct((1, 1), jnp.float32),
-            *[jax.ShapeDtypeStruct((orphans, cols), jnp.float32)] * 3,
-        ),
-        in_specs=[SMEM] * 3 + [VMEM] * 4,
-        out_specs=(VMEM,) * 6,
-        compiler_params=room(16),
+        out_shape=out_shape,
+        grid_spec=pltpu.PrefetchScalarGridSpec(
+            num_scalar_prefetch=3,
+            grid=(1,),
+            in_specs=[whole(names), whole(hidden), whole(o_grad)]
+            + [column_block(away, z) for away in aways for z in range(outer)],
+            out_specs=[whole(out) for out in out_shape],
+        ),
+        compiler_params=room(48),
         cost_estimate=terms_cost(shape, depth),
-    )(order, place, me, names, hidden, grad, o_grad)
+    )(order, place, me, names, hidden, o_grad, *[grad] * blocks)
 
 
 def other_terms(aways, order, place, weight, factor, hidden, grad, o_grad):
@@ -183,7 +200,8 @@
         order_ref, place_ref, weight_ref, factor_ref, hidden_ref, grad_ref, o_grad_ref, ring_ref
     ):
         write_terms(
-            aways, order_ref, place_ref[0], hidden_ref, grad_ref, o_grad_ref,
+            aways, order_ref, place_ref[0], hidden_ref,
+            lambda turn, z, at: grad_ref[:, at], o_grad_ref,
             weight_ref[:1], factor_ref[...], ring_ref,
         )
 

time: 97.4 us -> 96.6 us (level)
  local copies, waits for them, and re-layouts: 3.26 us -> 1.08 us
  Pallas kernels: 11.9 us -> 13.2 us
    unnamed x10, local copies, waits for them, and re-layouts: 3.26 us -> 1.08 us
    pallas_call x1, Pallas kernels: 2.14 us -> 3.43 us  [second_terms(): pl.pallas_call(kernel, name='second_terms', out_shape=out_shape, grid_spe...]
  transfers between devices with their start and end apart: 9 -> 9, of which waited for: 7 -> 7; matrix products, arithmetic and copies ran while one was open for 1% -> 1% of each run, Pallas kernels for 7% -> 9%
where the time goes in v3:
time: 96.6 us; the launch traced here: 96 us
  starting transfers between devices  38.4 us (40%)
  waiting for transfers between devices  29.5 us (31%)
  Pallas kernels  13.2 us (14%)
  blocking collectives  11.8 us (12%)
  between operations  1.49 us (2%)
  local copies, waits for them, and re-layouts  1.08 us (1%)
    ppermute x8, starting transfers between devices, shifted(): lax.ppermute(array, 'dp_1', [(i, (i + by) % size) for i in range(size)])  24.1 us
    ppermute x8, waiting for transfers between devices, shifted(): lax.ppermute(array, 'dp_1', [(i, (i + by) % size) for i in range(size)])  20.5 us
    all_to_all x1, starting transfers between devices, exchanged(): return lax.all_to_all(array, axis, split_axis=0, concat_axis=0, tiled=True)  14.3 us
    all_to_all x1, blocking collectives, exchanged(): return lax.all_to_all(array, axis, split_axis=0, concat_axis=0, tiled=True)  11.8 us
    all_to_all x1, waiting for transfers between devices, exchanged(): return lax.all_to_all(array, axis, split_axis=0, concat_axis=0, tiled=True)  8.91 us
    pallas_call x1, Pallas kernels, first_message(): pl.pallas_call(kernel, name='first_message', out_shape=[jax.ShapeDtypeStr...  3.64 us
    pallas_call x1, Pallas kernels, second_terms(): pl.pallas_call(kernel, name='second_terms', out_shape=out_shape, grid_spe...  3.43 us
    pallas_call x7, Pallas kernels, ring_sum(): pl.pallas_call(kernel, out_shape=jax.ShapeDtypeStruct((outer, rows, cols)...  2.79 us
  transfers between devices with their start and end apart: 9, of which 7 were waited for; matrix products, arithmetic and copies ran while one was open for 1% of the time, Pallas kernels for 9%

profile of v3, /device:TPU:64, one launch (start us, length us, event | category | flops | bytes accessed | tf_op | source)
XLA Modules:
  0.0 96.0 jit_solution(6518031907799374138)
XLA Ops:
  0.6 0.0 copy-start.4
  0.6 0.0 copy-start.1
  0.7 0.0 copy-start.3
  0.7 3.6 %first_message.1 = (bf16[448,544]{1,0:T(8,128)(2,1)}, bf16[4,320,128]{2,1,0:T(8,128)(2,1)}, bf16[4,256,128]{2,1,0:T(8,128)(2,1)}) custom-call(s32[32]{0:T(128)} %order_ref.5, s32[1]{0:T(128)} %bitcast.place_ref, bf16[448,512]{1,0:T(8,128)(2,1)} %gate_ref.1, bf16[448,512]{1,0:T(8,128)(2,1)} %up_ref.1, bf16[32,448]{1,0:T(8,128)(2,1)} %bitcast.10, ...), custom_call_target="tpu_custom_call" | custom-call | flops 234881024 | bytes 1835008 | tf_op jit(solution)/shard_map/first_message/pallas_call | solution.py:71
  4.3 5.4 %collective-permute-start.4 = (bf16[4,256,128]{2,1,0:T(8,128)(2,1)}, bf16[4,256,128]{2,1,0:T(8,128)(2,1)S(1)}, u32[]{:S(2)}, u32[]{:S(2)}) collective-permute-start(bf16[4,256,128]{2,1,0:T(8,128)(2,1)} %get-tuple-element.17), channel_id=1, source_target_pairs={{0,224},{32,0},{64,32},{96,64},{128,96},{160,128},{192,160},{224,1... | collective-permute-start | bytes 786440 | tf_op jit(solution)/shard_map/ppermute | solution.py:288
  9.7 1.9 %collective-permute-start = (bf16[4,320,128]{2,1,0:T(8,128)(2,1)}, bf16[4,320,128]{2,1,0:T(8,128)(2,1)S(1)}, u32[]{:S(2)}, u32[]{:S(2)}) collective-permute-start(bf16[4,320,128]{2,1,0:T(8,128)(2,1)} %get-tuple-element.15), channel_id=1, source_target_pairs={{0,32},{32,64},{64,96},{96,128},{128,160},{160,192},{192,224},{224... | collective-permute-start | bytes 983048 | tf_op jit(solution)/shard_map/ppermute | solution.py:288
  12.3 0.0 copy-done.4
  12.3 0.6 fusion
  12.9 14.3 %all-to-all-start = ((f32[32,1,32]{2,1,0:T(1,128)}), f32[32,1,32]{2,1,0:T(1,128)S(1)}, u32[]{:S(2)}, u32[]{:S(2)}) async-start(f32[32,1,32]{2,1,0:T(1,128)} %fusion), calls=%async_computation | async-start | bytes 32768 | tf_op jit(solution)/shard_map/all_to_all | solution.py:292
  27.3 8.9 %all-to-all-done = f32[32,1,32]{2,1,0:T(1,128)S(1)} async-done(((f32[32,1,32]{2,1,0:T(1,128)}), f32[32,1,32]{2,1,0:T(1,128)S(1)}, u32[]{:S(2)}, u32[]{:S(2)}) %all-to-all-start) | async-done | bytes 4128 | tf_op jit(solution)/shard_map/all_to_all | solution.py:292
  36.2 0.0 copy-done.1
  36.2 0.0 copy-done.3
  36.2 0.0 copy-start.2
  36.2 1.1 %copy-done.2 = bf16[448,544]{1,0:T(8,128)(2,1)S(1)} copy-done((bf16[448,544]{1,0:T(8,128)(2,1)S(1)}, bf16[448,544]{1,0:T(8,128)(2,1)}, u32[]{:S(2)}) %copy-start.2) | copy-done | bytes 487448
  37.2 3.4 %second_terms.1 = (f32[2,4,448,128]{3,2,1,0:T(8,128)S(1)}, f32[3,128]{1,0:T(4,128)S(1)}, f32[1,1]{1,0:T(1,128)}, f32[32,128]{1,0:T(8,128)S(1)}, f32[32,128]{1,0:T(8,128)S(1)}, /*index=5*/f32[32,128]{1,0:T(8,128)S(1)}) custom-call(s32[32]{0:T(128)S(1)} %copy-done.3, s32[1]{0:T(128)} %bitcast.place_ref, s32[1]{0:T(128)} %bitcast.1.me_ref, ...), custom_call_target="tpu_custom_call" | custom-call | flops 499122176 | bytes 2949120 | tf_op jit(solution)/shard_map/second_terms/pallas_call | solution.py:179
  40.7 0.0 copy-start
  40.7 0.0 collective-permute-done.4.refs_0_
  40.7 0.5 shard_map.107
  41.2 2.6 %collective-permute-start.5 = (bf16[4,448,128]{2,1,0:T(8,128)(2,1)S(1)}, bf16[4,448,128]{2,1,0:T(8,128)(2,1)S(1)}, u32[]{:S(2)}, u32[]{:S(2)}) collective-permute-start(bf16[4,448,128]{2,1,0:T(8,128)(2,1)S(1)} %shard_map.107), channel_id=1, source_target_pairs={{0,224},{32,0},{64,32},{96,64},{128,96},{160,128},{192,160},{224,1... | collective-permute-start | bytes 1376264 | tf_op jit(solution)/shard_map/ppermute | solution.py:288
  43.9 0.0 collective-permute-done.refs_0_
  43.9 0.6 shard_map.104
  44.4 3.4 %collective-permute-start.1 = (bf16[4,448,128]{2,1,0:T(8,128)(2,1)S(1)}, bf16[4,448,128]{2,1,0:T(8,128)(2,1)S(1)}, u32[]{:S(2)}, u32[]{:S(2)}) collective-permute-start(bf16[4,448,128]{2,1,0:T(8,128)(2,1)S(1)} %shard_map.104), channel_id=1, source_target_pairs={{0,32},{32,64},{64,96},{96,128},{128,160},{160,192},{192,224},{224... | collective-permute-start | bytes 1376264 | tf_op jit(solution)/shard_map/ppermute | solution.py:288
  47.8 0.0 copy-done
  47.8 2.6 %other_terms.1.ring_ref = f32[5,4,448,128]{3,2,1,0:T(8,128)S(1)} custom-call(s32[32]{0:T(128)S(1)} %copy-done.3, s32[1]{0:T(128)} %bitcast.place_ref, f32[3,128]{1,0:T(4,128)S(1)} %get-tuple-element.12.weight_ref.refs_1_, f32[32,128]{1,0:T(8,128)S(1)} %get-tuple-element.13.factor_ref, bf16[448,544]{1,0:T(8,128)(2,1)S(1)} %copy-done.2, ...), custom_call_target="tpu_custom_call" | custom-call | flops 1247805440 | bytes 7372800 | tf_op jit(solution)/shard_map/other_terms/pallas_call | solution.py:208
  50.4 3.3 %collective-permute-done.5.refs_0_ = bf16[4,448,128]{2,1,0:T(8,128)(2,1)S(1)} collective-permute-done((bf16[4,448,128]{2,1,0:T(8,128)(2,1)S(1)}, bf16[4,448,128]{2,1,0:T(8,128)(2,1)S(1)}, u32[]{:S(2)}, u32[]{:S(2)}) %collective-permute-start.5) | collective-permute-done | bytes 458784 | tf_op jit(solution)/shard_map/ppermute | solution.py:288
  53.7 0.3 shard_map.108
  54.1 2.5 %collective-permute-start.6 = (bf16[4,448,128]{2,1,0:T(8,128)(2,1)S(1)}, bf16[4,448,128]{2,1,0:T(8,128)(2,1)S(1)}, u32[]{:S(2)}, u32[]{:S(2)}) collective-permute-start(bf16[4,448,128]{2,1,0:T(8,128)(2,1)S(1)} %shard_map.108), channel_id=1, source_target_pairs={{0,224},{32,0},{64,32},{96,64},{128,96},{160,128},{192,160},{224,1... | collective-permute-start | bytes 1376264 | tf_op jit(solution)/shard_map/ppermute | solution.py:288
  56.6 0.5 collective-permute-done.1.refs_0_
  57.1 0.3 shard_map.105
  57.4 3.1 %collective-permute-start.2 = (bf16[4,448,128]{2,1,0:T(8,128)(2,1)S(1)}, bf16[4,448,128]{2,1,0:T(8,128)(2,1)S(1)}, u32[]{:S(2)}, u32[]{:S(2)}) collective-permute-start(bf16[4,448,128]{2,1,0:T(8,128)(2,1)S(1)} %shard_map.105), channel_id=1, source_target_pairs={{0,32},{32,64},{64,96},{96,128},{128,160},{160,192},{192,224},{224... | collective-permute-start | bytes 1376264 | tf_op jit(solution)/shard_map/ppermute | solution.py:288
  60.5 6.8 %collective-permute-done.6.refs_0_ = bf16[4,448,128]{2,1,0:T(8,128)(2,1)S(1)} collective-permute-done((bf16[4,448,128]{2,1,0:T(8,128)(2,1)S(1)}, bf16[4,448,128]{2,1,0:T(8,128)(2,1)S(1)}, u32[]{:S(2)}, u32[]{:S(2)}) %collective-permute-start.6) | collective-permute-done | bytes 458784 | tf_op jit(solution)/shard_map/ppermute | solution.py:288
  67.3 0.3 shard_map.109
  67.6 2.8 %collective-permute-start.7 = (bf16[4,448,128]{2,1,0:T(8,128)(2,1)S(1)}, bf16[4,448,128]{2,1,0:T(8,128)(2,1)S(1)}, u32[]{:S(2)}, u32[]{:S(2)}) collective-permute-start(bf16[4,448,128]{2,1,0:T(8,128)(2,1)S(1)} %shard_map.109), channel_id=1, source_target_pairs={{0,224},{32,0},{64,32},{96,64},{128,96},{160,128},{192,160},{224,1... | collective-permute-start | bytes 1376264 | tf_op jit(solution)/shard_map/ppermute | solution.py:288
  70.4 0.8 collective-permute-done.2.refs_0_
  71.3 0.3 shard_map.106
  71.6 2.5 %collective-permute-start.3 = (bf16[4,448,128]{2,1,0:T(8,128)(2,1)S(1)}, bf16[4,448,128]{2,1,0:T(8,128)(2,1)S(1)}, u32[]{:S(2)}, u32[]{:S(2)}) collective-permute-start(bf16[4,448,128]{2,1,0:T(8,128)(2,1)S(1)} %shard_map.106), channel_id=1, source_target_pairs={{0,32},{32,64},{64,96},{96,128},{128,160},{160,192},{192,224},{224... | collective-permute-start | bytes 1376264 | tf_op jit(solution)/shard_map/ppermute | solution.py:288
  74.0 4.0 %collective-permute-done.7.refs_1_ = bf16[4,448,128]{2,1,0:T(8,128)(2,1)S(1)} collective-permute-done((bf16[4,448,128]{2,1,0:T(8,128)(2,1)S(1)}, bf16[4,448,128]{2,1,0:T(8,128)(2,1)S(1)}, u32[]{:S(2)}, u32[]{:S(2)}) %collective-permute-start.7) | collective-permute-done | bytes 458784 | tf_op jit(solution)/shard_map/ppermute | solution.py:288
  78.0 5.2 %collective-permute-done.3.refs_0_ = bf16[4,448,128]{2,1,0:T(8,128)(2,1)S(1)} collective-permute-done((bf16[4,448,128]{2,1,0:T(8,128)(2,1)S(1)}, bf16[4,448,128]{2,1,0:T(8,128)(2,1)S(1)}, u32[]{:S(2)}, u32[]{:S(2)}) %collective-permute-start.3) | collective-permute-done | bytes 458784 | tf_op jit(solution)/shard_map/ppermute | solution.py:288
  83.2 0.4 shard_map.110
  83.5 11.8 %all_to_all.10.near_ref = bf16[4,448,128]{2,1,0:T(8,128)(2,1)S(1)} all-to-all(bf16[4,448,128]{2,1,0:T(8,128)(2,1)S(1)} %shard_map.110), channel_id=1, replica_groups=mesh['dp_0'=4,'dp_1'=8,'tensor'=32] {'dp_0'}, dimensions={0} | all-to-all | bytes 917504 | tf_op jit(solution)/shard_map/all_to_all | solution.py:292
  95.3 0.7 total_of.1
  (1 shorter events, 0.0 us)
Async XLA Ops:
  0.6 11.6 %copy-start.4 = (s32[32,1]{0,1:T(1,128)S(1)}, s32[32,1]{0,1:T(1,128)}, u32[]{:S(2)}) copy-start(s32[32,1]{0,1:T(1,128)} %param.16) | copy-start | bytes 388
  0.6 35.5 %copy-start.1 = (bf16[32,4096]{1,0:T(8,128)(2,1)S(1)}, bf16[32,4096]{1,0:T(8,128)(2,1)}, u32[]{:S(2)}) copy-start(bf16[32,4096]{1,0:T(8,128)(2,1)} %o_grad_ref.3) | copy-start | bytes 786436
  0.7 35.5 %copy-start.3 = (s32[32]{0:T(128)S(1)}, s32[32]{0:T(128)}, u32[]{:S(2)}) copy-start(s32[32]{0:T(128)} %order_ref.5) | copy-start | bytes 388
  4.3 36.4 %collective-permute-start.4 = (bf16[4,256,128]{2,1,0:T(8,128)(2,1)}, bf16[4,256,128]{2,1,0:T(8,128)(2,1)S(1)}, u32[]{:S(2)}, u32[]{:S(2)}) collective-permute-start(bf16[4,256,128]{2,1,0:T(8,128)(2,1)} %get-tuple-element.17), channel_id=1, source_target_pairs={{0,224},{32,0},{64,32},{96,64},{128,96},{160,128},{192,160},{224,1... | collective-permute-start | bytes 786440 | tf_op jit(solution)/shard_map/ppermute | solution.py:288
  9.7 34.2 %collective-permute-start = (bf16[4,320,128]{2,1,0:T(8,128)(2,1)}, bf16[4,320,128]{2,1,0:T(8,128)(2,1)S(1)}, u32[]{:S(2)}, u32[]{:S(2)}) collective-permute-start(bf16[4,320,128]{2,1,0:T(8,128)(2,1)} %get-tuple-element.15), channel_id=1, source_target_pairs={{0,32},{32,64},{64,96},{96,128},{128,160},{160,192},{192,224},{224... | collective-permute-start | bytes 983048 | tf_op jit(solution)/shard_map/ppermute | solution.py:288
  12.9 23.3 %all-to-all-start = ((f32[32,1,32]{2,1,0:T(1,128)}), f32[32,1,32]{2,1,0:T(1,128)S(1)}, u32[]{:S(2)}, u32[]{:S(2)}) async-start(f32[32,1,32]{2,1,0:T(1,128)} %fusion), calls=%async_computation | async-start | bytes 32768 | tf_op jit(solution)/shard_map/all_to_all | solution.py:292
  36.2 1.1 %copy-start.2 = (bf16[448,544]{1,0:T(8,128)(2,1)S(1)}, bf16[448,544]{1,0:T(8,128)(2,1)}, u32[]{:S(2)}) copy-start(bf16[448,544]{1,0:T(8,128)(2,1)} %get-tuple-element.11.hidden_ref) | copy-start | bytes 1462276
  40.7 7.1 %copy-start = (bf16[512,4096]{1,0:T(8,128)(2,1)S(1)}, bf16[512,4096]{1,0:T(8,128)(2,1)}, u32[]{:S(2)}) copy-start(bf16[512,4096]{1,0:T(8,128)(2,1)} %grad_ref.1) | copy-start | bytes 12582916
  41.2 12.5 %collective-permute-start.5 = (bf16[4,448,128]{2,1,0:T(8,128)(2,1)S(1)}, bf16[4,448,128]{2,1,0:T(8,128)(2,1)S(1)}, u32[]{:S(2)}, u32[]{:S(2)}) collective-permute-start(bf16[4,448,128]{2,1,0:T(8,128)(2,1)S(1)} %shard_map.107), channel_id=1, source_target_pairs={{0,224},{32,0},{64,32},{96,64},{128,96},{160,128},{192,160},{224,1... | collective-permute-start | bytes 1376264 | tf_op jit(solution)/shard_map/ppermute | solution.py:288
  44.4 12.7 %collective-permute-start.1 = (bf16[4,448,128]{2,1,0:T(8,128)(2,1)S(1)}, bf16[4,448,128]{2,1,0:T(8,128)(2,1)S(1)}, u32[]{:S(2)}, u32[]{:S(2)}) collective-permute-start(bf16[4,448,128]{2,1,0:T(8,128)(2,1)S(1)} %shard_map.104), channel_id=1, source_target_pairs={{0,32},{32,64},{64,96},{96,128},{128,160},{160,192},{192,224},{224... | collective-permute-start | bytes 1376264 | tf_op jit(solution)/shard_map/ppermute | solution.py:288
  54.1 13.2 %collective-permute-start.6 = (bf16[4,448,128]{2,1,0:T(8,128)(2,1)S(1)}, bf16[4,448,128]{2,1,0:T(8,128)(2,1)S(1)}, u32[]{:S(2)}, u32[]{:S(2)}) collective-permute-start(bf16[4,448,128]{2,1,0:T(8,128)(2,1)S(1)} %shard_map.108), channel_id=1, source_target_pairs={{0,224},{32,0},{64,32},{96,64},{128,96},{160,128},{192,160},{224,1... | collective-permute-start | bytes 1376264 | tf_op jit(solution)/shard_map/ppermute | solution.py:288
  57.4 13.8 %collective-permute-start.2 = (bf16[4,448,128]{2,1,0:T(8,128)(2,1)S(1)}, bf16[4,448,128]{2,1,0:T(8,128)(2,1)S(1)}, u32[]{:S(2)}, u32[]{:S(2)}) collective-permute-start(bf16[4,448,128]{2,1,0:T(8,128)(2,1)S(1)} %shard_map.105), channel_id=1, source_target_pairs={{0,32},{32,64},{64,96},{96,128},{128,160},{160,192},{192,224},{224... | collective-permute-start | bytes 1376264 | tf_op jit(solution)/shard_map/ppermute | solution.py:288
  67.6 10.4 %collective-permute-start.7 = (bf16[4,448,128]{2,1,0:T(8,128)(2,1)S(1)}, bf16[4,448,128]{2,1,0:T(8,128)(2,1)S(1)}, u32[]{:S(2)}, u32[]{:S(2)}) collective-permute-start(bf16[4,448,128]{2,1,0:T(8,128)(2,1)S(1)} %shard_map.109), channel_id=1, source_target_pairs={{0,224},{32,0},{64,32},{96,64},{128,96},{160,128},{192,160},{224,1... | collective-permute-start | bytes 1376264 | tf_op jit(solution)/shard_map/ppermute | solution.py:288
  71.6 11.6 %collective-permute-start.3 = (bf16[4,448,128]{2,1,0:T(8,128)(2,1)S(1)}, bf16[4,448,128]{2,1,0:T(8,128)(2,1)S(1)}, u32[]{:S(2)}, u32[]{:S(2)}) collective-permute-start(bf16[4,448,128]{2,1,0:T(8,128)(2,1)S(1)} %shard_map.106), channel_id=1, source_target_pairs={{0,32},{32,64},{64,96},{96,128},{128,160},{160,192},{192,224},{224... | collective-permute-start | bytes 1376264 | tf_op jit(solution)/shard_map/ppermute | solution.py:288
